TPU v7x, 128 devices: a whole 4x4x4 slice. The times are simulated.
128 devices in a mesh: gx: 8 (over y, core), gy: 16 (over z, x).
Axes of the slice: x: 4, y: 4, z: 4, core: 2. Of those that a mesh axis runs over, the one named last changes fastest.
Arguments:
- raw_window: float32 [8192, 16384], P('gx', 'gy'), may hold values from -6 to 6
- source_ids: int32 [256], P(('gx', 'gy')), may hold values from 0 to 8191, as said below
- pair_source: int32 [16384], P(('gx', 'gy')), may hold values from 0 to 255
- pair_holder: int32 [16384, 1], P(('gx', 'gy')), may hold values from 0 to 127; in each aligned block of 128 rows (0 to 127, 128 to 255, ...) at most 2 rows name the same one
- pair_receiver: int32 [16384], P(('gx', 'gy')), may hold values from 0 to 63
Outputs:
- correlations: float32 [16384, 512], P(('gx', 'gy'))
Inputs may be any that keep to these rules, and one draw needn't show every extreme that they name: The ids are distinct, and source k is a channel of the device that holds channels from (k // 2) * 64 on: source_ids[k] // 64 == k // 2. `pair_holder`: among the 128 pairs of one device, at most 2 name the same holder, a bound that some block reaches; every device is named by some pair.
All inputs are finite; a program needn't handle non-finite values.
Results may differ from a plain program's by a relative error of at most 0.0095.
Values may be sent and summed in bfloat16 or wider, within the bound.
No kernel may reach another device: no remote copies, remote signals or barrier semaphores. Data moves between devices by JAX's collectives and lax.ppermute only.
A program may use at most 128 MiB of HBM per device.

v0:
```python
import math

import jax
import jax.numpy as jnp
from jax import lax
from jax.sharding import PartitionSpec as P

NBIN = 2048
SEGLEN = 4096
NSEG = 4
BAND = 64
NLAG = 512


def split_table(table):
    upper = table.astype(jnp.bfloat16)
    lower = (table - upper.astype(jnp.float32)).astype(jnp.bfloat16)
    return (upper, lower)


def inverse_table():
    bins = jnp.arange(NBIN, dtype=jnp.int32)
    lags = (jnp.arange(NLAG, dtype=jnp.int32) - NLAG // 2) % SEGLEN
    phase = bins[:, None] * lags[None, :] % SEGLEN
    angle = phase.astype(jnp.float32) * (2.0 * math.pi / SEGLEN)
    weight = jnp.where(bins == 0, 1.0, 2.0).astype(jnp.float32) * (0.5 / math.sqrt(NSEG * NBIN))
    return jnp.concatenate(
        [weight[:, None] * jnp.cos(angle), -weight[:, None] * jnp.sin(angle)], axis=0
    )


def whiten_block(seg_rows, block, width):
    times = jnp.arange(SEGLEN, dtype=jnp.int32)
    bins = block * width + jnp.arange(width, dtype=jnp.int32)
    phase = times[:, None] * bins[None, :] % SEGLEN
    angle = phase.astype(jnp.float32) * (2.0 * math.pi / SEGLEN)
    upper, lower = split_table(jnp.concatenate([jnp.cos(angle), -jnp.sin(angle)], axis=1))
    spectrum = jnp.dot(seg_rows, upper, preferred_element_type=jnp.float32)
    spectrum = spectrum + jnp.dot(seg_rows, lower, preferred_element_type=jnp.float32)
    real_part = spectrum[:, :width]
    imag_part = spectrum[:, width:]
    count = seg_rows.shape[0]
    power = (real_part * real_part + imag_part * imag_part).reshape(count, width // BAND, BAND)
    level = jnp.repeat(jnp.sqrt(jnp.mean(power, axis=2) + 1e-06), BAND, axis=1)
    return jnp.stack([real_part / level, imag_part / level], axis=1).astype(jnp.bfloat16)


def correlate(source_rows, receiver_rows, upper, lower):
    first = source_rows.astype(jnp.float32)
    second = receiver_rows.astype(jnp.float32)
    real_part = jnp.sum(first[:, :, 0] * second[:, :, 0] + first[:, :, 1] * second[:, :, 1], axis=1)
    imag_part = jnp.sum(first[:, :, 1] * second[:, :, 0] - first[:, :, 0] * second[:, :, 1], axis=1)
    cross = jnp.concatenate([real_part, imag_part], axis=1).astype(jnp.bfloat16)
    result = jnp.dot(cross, upper, preferred_element_type=jnp.float32)
    return result + jnp.dot(cross, lower, preferred_element_type=jnp.float32)


def body(raw_window, source_ids, pair_source, pair_holder, pair_receiver):
    groups = lax.axis_size("gy")
    devices = lax.axis_size("gx") * groups
    span = raw_window.shape[1]
    sample = (lax.axis_index("gy") * span + jnp.arange(span, dtype=jnp.int32)) % SEGLEN
    taper = jnp.sin(math.pi * (sample.astype(jnp.float32) + 0.5) / SEGLEN) ** 2
    tapered = (raw_window * taper[None, :]).astype(jnp.bfloat16)
    regrouped = lax.all_to_all(tapered, "gy", split_axis=0, concat_axis=1, tiled=True)
    channels = regrouped.shape[0]
    seg_rows = regrouped.reshape(channels * NSEG, SEGLEN)
    width = min(256, NBIN)

    def one_block(block):
        return whiten_block(seg_rows, block, width)

    blocks = lax.map(one_block, jnp.arange(NBIN // width, dtype=jnp.int32))
    whitened = jnp.transpose(blocks, (1, 2, 0, 3)).reshape(channels, NSEG, 2, NBIN)
    here = lax.axis_index("gx") * groups + lax.axis_index("gy")
    mine = jnp.take(whitened, source_ids - here * channels, axis=0)
    sources = lax.all_gather(mine, ("gx", "gy"), axis=0, tiled=True)
    pairs = pair_source.shape[0]
    slots = 2 * pairs // devices
    holder = pair_holder[:, 0]
    onehot = (holder[:, None] == jnp.arange(devices, dtype=jnp.int32)[None, :]).astype(jnp.int32)
    earlier = jnp.cumsum(onehot, axis=0) - onehot
    rank = jnp.sum(earlier * onehot, axis=1)
    slot = holder * slots + rank
    wanted = jnp.stack([pair_receiver, pair_source], axis=1)
    outgoing = jnp.full((devices * slots, 2), -1, jnp.int32).at[slot].set(wanted)
    incoming = lax.all_to_all(outgoing, ("gx", "gy"), split_axis=0, concat_axis=0, tiled=True)
    asked_receiver = jnp.clip(incoming[:, 0], 0, channels - 1)
    upper, lower = split_table(inverse_table())
    picked = jnp.take(whitened, asked_receiver, axis=0)
    returned = lax.all_to_all(picked, ("gx", "gy"), split_axis=0, concat_axis=0, tiled=True)
    receiver_rows = jnp.take(returned, slot, axis=0)
    source_rows = jnp.take(sources, pair_source, axis=0)
    return correlate(source_rows, receiver_rows, upper, lower)


def solution(mesh):
    return jax.shard_map(
        body,
        mesh=mesh,
        in_specs=(
            P("gx", "gy"),
            P(("gx", "gy")),
            P(("gx", "gy")),
            P(("gx", "gy"), None),
            P(("gx", "gy")),
        ),
        out_specs=P(("gx", "gy"), None),
        check_vma=False,
    )
```

profile of v0, /device:TPU:5, one launch (start us, length us, event | category | flops | bytes accessed | tf_op | source)
XLA Modules:
  0.0 458.6 jit_solution(11175273409968126107)
XLA Ops:
  6.6 4.1 multiply_convert_fusion
  10.7 7.7 %all-to-all-start = ((bf16[16,64,1024]{2,1,0:T(8,128)(2,1)}), bf16[16,64,1024]{2,1,0:T(8,128)(2,1)S(1)}, u32[]{:S(2)}, u32[]{:S(2)}) async-start(bf16[16,64,1024]{2,1,0:T(8,128)(2,1)} %bitcast.55), calls=%async_computation | async-start | bytes 4194304 | tf_op jit(solution)/shard_map/all_to_all | solution.py:65
  18.5 28.3 %all-to-all-done = bf16[16,64,1024]{2,1,0:T(8,128)(2,1)S(1)} async-done(((bf16[16,64,1024]{2,1,0:T(8,128)(2,1)}), bf16[16,64,1024]{2,1,0:T(8,128)(2,1)S(1)}, u32[]{:S(2)}, u32[]{:S(2)}) %all-to-all-start) | async-done | bytes 2097184 | tf_op jit(solution)/shard_map/all_to_all | solution.py:65
  46.8 2.5 copy.32
  49.3 3.6 reshape.135
  52.9 171.0 %while.12 = (s32[]{:T(128)}, bf16[8,256,2,256]{1,3,2,0:T(8,128)(2,1)}, s32[8]{0:T(128)S(1)}, bf16[256,4096]{1,0:T(8,128)(2,1)S(1)}, s32[]{:T(128)}, /*index=5*/s32[1]{0:T(128)}) while((s32[]{:T(128)}, bf16[8,256,2,256]{1,3,2,0:T(8,128)(2,1)}, s32[8]{0:T(128)S(1)}, bf16[256,4096]{1,0:T(8,128)(2,1)S(1)}, s32[]{:T(128)}, ...), condition=%wide.region_2.3_spmd, body=%wide.region_0.2_spmd.sunk | while | flops 2183267584 | bytes 32787040 | solution.py:73
  54.2 16.5 %fusion.59 = (f32[4096,256]{1,0:T(8,128)S(1)}, f32[4096,256]{1,0:T(8,128)S(1)}) fusion(s32[256]{0:T(256)S(1)} %iota_add_fusion.2), kind=kLoop, calls=%fused_computation.20.clone.1 | loop fusion | flops 15728640 | bytes 8389632 | tf_op jit(solution)/shard_map/while/body/eval_jaxpr/cos | solution.py:37
  75.5 16.5 %fusion.59 = (f32[4096,256]{1,0:T(8,128)S(1)}, f32[4096,256]{1,0:T(8,128)S(1)}) fusion(s32[256]{0:T(256)S(1)} %iota_add_fusion.2), kind=kLoop, calls=%fused_computation.20.clone.1 | loop fusion | flops 15728640 | bytes 8389632 | tf_op jit(solution)/shard_map/while/body/eval_jaxpr/cos | solution.py:37
  96.9 16.5 %fusion.59 = (f32[4096,256]{1,0:T(8,128)S(1)}, f32[4096,256]{1,0:T(8,128)S(1)}) fusion(s32[256]{0:T(256)S(1)} %iota_add_fusion.2), kind=kLoop, calls=%fused_computation.20.clone.1 | loop fusion | flops 15728640 | bytes 8389632 | tf_op jit(solution)/shard_map/while/body/eval_jaxpr/cos | solution.py:37
  114.8 1.4 fusion.61
  118.3 16.5 %fusion.59 = (f32[4096,256]{1,0:T(8,128)S(1)}, f32[4096,256]{1,0:T(8,128)S(1)}) fusion(s32[256]{0:T(256)S(1)} %iota_add_fusion.2), kind=kLoop, calls=%fused_computation.20.clone.1 | loop fusion | flops 15728640 | bytes 8389632 | tf_op jit(solution)/shard_map/while/body/eval_jaxpr/cos | solution.py:37
  139.6 16.5 %fusion.59 = (f32[4096,256]{1,0:T(8,128)S(1)}, f32[4096,256]{1,0:T(8,128)S(1)}) fusion(s32[256]{0:T(256)S(1)} %iota_add_fusion.2), kind=kLoop, calls=%fused_computation.20.clone.1 | loop fusion | flops 15728640 | bytes 8389632 | tf_op jit(solution)/shard_map/while/body/eval_jaxpr/cos | solution.py:37
  161.0 16.5 %fusion.59 = (f32[4096,256]{1,0:T(8,128)S(1)}, f32[4096,256]{1,0:T(8,128)S(1)}) fusion(s32[256]{0:T(256)S(1)} %iota_add_fusion.2), kind=kLoop, calls=%fused_computation.20.clone.1 | loop fusion | flops 15728640 | bytes 8389632 | tf_op jit(solution)/shard_map/while/body/eval_jaxpr/cos | solution.py:37
  178.9 1.4 fusion.61
  182.4 16.5 %fusion.59 = (f32[4096,256]{1,0:T(8,128)S(1)}, f32[4096,256]{1,0:T(8,128)S(1)}) fusion(s32[256]{0:T(256)S(1)} %iota_add_fusion.2), kind=kLoop, calls=%fused_computation.20.clone.1 | loop fusion | flops 15728640 | bytes 8389632 | tf_op jit(solution)/shard_map/while/body/eval_jaxpr/cos | solution.py:37
  200.3 1.4 fusion.61
  203.8 16.5 %fusion.59 = (f32[4096,256]{1,0:T(8,128)S(1)}, f32[4096,256]{1,0:T(8,128)S(1)}) fusion(s32[256]{0:T(256)S(1)} %iota_add_fusion.2), kind=kLoop, calls=%fused_computation.20.clone.1 | loop fusion | flops 15728640 | bytes 8389632 | tf_op jit(solution)/shard_map/while/body/eval_jaxpr/cos | solution.py:37
  223.9 4.7 %copy.33 = bf16[256,2,8,256]{3,2,1,0:T(8,128)(2,1)} copy(bf16[256,2,8,256]{0,3,1,2:T(8,128)(2,1)} %bitcast.8) | data formatting | bytes 4194304 | tf_op jit(solution)/shard_map/transpose | solution.py:74
  228.7 2.5 reshape.136
  235.1 18.1 %all_to_all.33 = s32[128,2,2]{1,2,0:T(2,128)S(1)} all-to-all(s32[128,2,2]{1,2,0:T(2,128)S(1)} %copy.36), channel_id=1, replica_groups=mesh['gx'=8,'gy'=16] {'gx','gy'}, dimensions={0} | all-to-all | bytes 4096 | tf_op jit(solution)/shard_map/all_to_all | solution.py:87
  253.5 2.7 copy.38
  256.1 12.5 %gather_fusion.1 = bf16[256,4,2,2048]{3,1,2,0:T(4,128)(2,1)} fusion(bf16[64,4,2,2048]{3,1,2,0:T(4,128)(2,1)S(1)} %copy.38, s32[1024]{0:T(1024)S(1)} %pad_clamp_fusion.1), kind=kCustom, calls=%fused_computation.3 | custom fusion | bytes 16778240 | tf_op jit(solution)/shard_map/jit(_take)/gather | solution.py:90
  268.7 8.6 %broadcast_select_fusion = bf16[256,4,2,2048]{3,1,2,0:T(4,128)(2,1)} fusion(bf16[256,4,2,2048]{3,1,2,0:T(4,128)(2,1)} %gather_fusion.1, pred[256]{0:T(512)(128)(4,1)S(1)} %get-tuple-element.75), kind=kLoop, calls=%fused_computation.36 | loop fusion | flops 4194304 | bytes 16777472 | tf_op jit(solution)/shard_map/jit(_take)/select_n | solution.py:90
  277.2 7.6 %all-to-all-start.2 = ((bf16[256,4,2,2048]{3,1,2,0:T(4,128)(2,1)}), bf16[256,4,2,2048]{3,1,2,0:T(4,128)(2,1)}, u32[]{:S(2)}, u32[]{:S(2)}) async-start(bf16[256,4,2,2048]{3,1,2,0:T(4,128)(2,1)} %broadcast_select_fusion), calls=%async_computation.2 | async-start | bytes 16777216 | tf_op jit(solution)/shard_map/all_to_all | solution.py:91
  285.0 18.2 %cosine_multiply_fusion = (f32[2048,512]{1,0:T(8,128)}, f32[2048,512]{1,0:T(8,128)}) fusion(s32[512]{0:T(512)S(1)} %add_select_fusion.3, f32[2048]{0:T(1024)S(1)} %get-tuple-element.83, f32[2048]{0:T(1024)S(1)} %get-tuple-element.84), kind=kLoop, calls=%fused_computation.48 | loop fusion | flops 16777216 | bytes 8407040 | tf_op jit(solution)/shard_map/mul | solution.py:28
  303.2 98.2 %all-to-all-done.2 = bf16[256,4,2,2048]{3,1,2,0:T(4,128)(2,1)} async-done(((bf16[256,4,2,2048]{3,1,2,0:T(4,128)(2,1)}), bf16[256,4,2,2048]{3,1,2,0:T(4,128)(2,1)}, u32[]{:S(2)}, u32[]{:S(2)}) %all-to-all-start.2) | async-done | bytes 8388640 | tf_op jit(solution)/shard_map/all_to_all | solution.py:91
  401.3 10.9 %gather_fusion.3 = bf16[128,4,2,2048]{3,1,2,0:T(4,128)(2,1)} fusion(bf16[256,4,2,2048]{3,1,2,0:T(4,128)(2,1)} %all-to-all-done.2, s32[1024]{0:T(1024)S(1)} %pad_clamp_fusion), kind=kCustom, calls=%fused_computation.1.clone | custom fusion | bytes 8389120 | tf_op jit(solution)/shard_map/jit(_take)/gather | solution.py:92
  412.2 7.0 %select_convert_fusion = f32[128,4,2,2048]{3,1,2,0:T(4,128)} fusion(bf16[128,4,2,2048]{3,1,2,0:T(4,128)(2,1)} %gather_fusion.3, pred[128]{0:T(512)(128)(4,1)S(1)} %get-tuple-element.73), kind=kLoop, calls=%fused_computation.45 | loop fusion | flops 4194304 | bytes 12583040 | tf_op jit(solution)/shard_map/convert_element_type | solution.py:50
  419.3 10.9 %gather_fusion.2 = bf16[128,4,2,2048]{3,1,2,0:T(4,128)(2,1)} fusion(bf16[256,4,2,2048]{3,1,2,0:T(4,128)(2,1)} %all-gather.2.cloned.1.call-done, s32[1024]{0:T(1024)S(1)} %pad_clamp_fusion.2), kind=kCustom, calls=%fused_computation.clone | custom fusion | bytes 8389120 | tf_op jit(solution)/shard_map/jit(_take)/gather | solution.py:93
  430.1 7.2 %select_convert_fusion.1 = f32[128,4,2,2048]{3,1,2,0:T(4,128)} fusion(bf16[128,4,2,2048]{3,1,2,0:T(4,128)(2,1)} %gather_fusion.2, pred[128]{0:T(512)(128)(4,1)S(1)} %compare_and_fusion.1), kind=kLoop, calls=%fused_computation.46 | loop fusion | flops 4194304 | bytes 12583040 | tf_op jit(solution)/shard_map/convert_element_type | solution.py:49
  437.3 12.0 %add_reduce_fusion = (bf16[128,2048]{1,0:T(8,128)(2,1)S(1)}, bf16[128,2048]{1,0:T(8,128)(2,1)S(1)}) fusion(f32[128,4,2,2048]{3,1,2,0:T(4,128)S(1)} %copy-done, f32[128,4,2,2048]{3,1,2,0:T(4,128)} %select_convert_fusion.1), kind=kLoop, calls=%fused_computation.52 | loop fusion | flops 7864320 | bytes 17825792 | tf_op jit(solution)/shard_map/reduce_sum | solution.py:51
  450.1 1.4 fusion.27
  (108 shorter events, 34.2 us)
Async XLA Ops:
  6.6 11.9 %copy-start.5 = (s32[2]{0:T(128)S(1)}, s32[2]{0:T(128)}, u32[]{:S(2)}) copy-start(s32[2]{0:T(128)} %param.10) | copy-start | bytes 28
  10.7 36.1 %all-to-all-start = ((bf16[16,64,1024]{2,1,0:T(8,128)(2,1)}), bf16[16,64,1024]{2,1,0:T(8,128)(2,1)S(1)}, u32[]{:S(2)}, u32[]{:S(2)}) async-start(bf16[16,64,1024]{2,1,0:T(8,128)(2,1)} %bitcast.55), calls=%async_computation | async-start | bytes 4194304 | tf_op jit(solution)/shard_map/all_to_all | solution.py:65
  18.4 400.8 %all-gather.2.cloned.1.call-start = ((), (), s32[]{:S(2)}) async-start(), calls=%async_computation.3 | async-start | bytes 8454144 | tf_op jit(solution)/shard_map/all_gather | solution.py:77
  223.9 8.8 %copy-start.4 = (s32[128,1]{0,1:T(1,128)S(1)}, s32[128,1]{0,1:T(1,128)}, u32[]{:S(2)}) copy-start(s32[128,1]{0,1:T(1,128)} %param.12) | copy-start | bytes 1540
  223.9 9.1 %copy-start.6 = (s32[128]{0:T(128)S(1)}, s32[128]{0:T(128)}, u32[]{:S(2)}) copy-start(s32[128]{0:T(128)} %param.13) | copy-start | bytes 1540
  223.9 9.1 %copy-start.7 = (s32[128]{0:T(128)S(1)}, s32[128]{0:T(128)}, u32[]{:S(2)}) copy-start(s32[128]{0:T(128)} %param.11) | copy-start | bytes 1540
  231.2 22.2 %copy-start.3 = (bf16[64,4,2,2048]{3,2,1,0:T(2,128)(2,1)}, bf16[64,4,2,2048]{3,2,1,0:T(2,128)(2,1)S(1)}, u32[]{:S(2)}) copy-start(bf16[64,4,2,2048]{3,2,1,0:T(2,128)(2,1)S(1)} %reshape.136) | copy-start | bytes 6291460
  277.2 124.1 %all-to-all-start.2 = ((bf16[256,4,2,2048]{3,1,2,0:T(4,128)(2,1)}), bf16[256,4,2,2048]{3,1,2,0:T(4,128)(2,1)}, u32[]{:S(2)}, u32[]{:S(2)}) async-start(bf16[256,4,2,2048]{3,1,2,0:T(4,128)(2,1)} %broadcast_select_fusion), calls=%async_computation.2 | async-start | bytes 16777216 | tf_op jit(solution)/shard_map/all_to_all | solution.py:91
  430.1 7.2 %copy-start = (f32[128,4,2,2048]{3,1,2,0:T(4,128)S(1)}, f32[128,4,2,2048]{3,1,2,0:T(4,128)}, u32[]{:S(2)}) copy-start(f32[128,4,2,2048]{3,1,2,0:T(4,128)} %select_convert_fusion) | copy-start | bytes 25165828
  437.3 12.0 %copy-start.1 = (f32[2048,512]{1,0:T(8,128)S(1)}, f32[2048,512]{1,0:T(8,128)}, u32[]{:S(2)}) copy-start(f32[2048,512]{1,0:T(8,128)} %get-tuple-element.81) | copy-start | bytes 12582916
  437.3 12.0 %copy-start.2 = (f32[2048,512]{1,0:T(8,128)S(1)}, f32[2048,512]{1,0:T(8,128)}, u32[]{:S(2)}) copy-start(f32[2048,512]{1,0:T(8,128)} %get-tuple-element.82) | copy-start | bytes 12582916
Sparse Core Ops, SparseCore 0:
  232.9 156.0 all-gather.1
where the time goes:
time: 461 us; the launch traced here: 459 us
  other arithmetic  197 us (43%)
  waiting for transfers between devices  127 us (28%)
  local copies, waits for them, and re-layouts  58.5 us (13%)
  matrix products  24.1 us (5%)
  blocking collectives  18.1 us (4%)
  starting transfers between devices  15.4 us (3%)
  between operations  13.9 us (3%)
  loops' own time  5.44 us (1%)
    cos x8, other arithmetic, whiten_block(): jnp.cos(angle)  132 us
    all_to_all x1, waiting for transfers between devices, body(): lax.all_to_all(picked, ('gx', 'gy'), split_axis=0, concat_axis=0, tiled=T...  98.2 us
    all_to_all x1, waiting for transfers between devices, body(): lax.all_to_all(tapered, 'gy', split_axis=0, concat_axis=1, tiled=True)  28.3 us
    mul x1, other arithmetic, inverse_table(): weight[:, None] * jnp.cos(angle)  18.2 us
    all_to_all x1, blocking collectives, body(): lax.all_to_all(outgoing, ('gx', 'gy'), split_axis=0, concat_axis=0, tiled...  18.1 us
    gather x1, local copies, waits for them, and re-layouts, body(): picked = jnp.take(whitened, asked_receiver, axis=0)  12.5 us
    reduce_sum x1, other arithmetic, correlate(): jnp.sum(first[:, :, 0] * second[:, :, 0] + first[:, :, 1] * second[:, :,...  12 us
    dot_general x8, matrix products, whiten_block(): spectrum = jnp.dot(seg_rows, upper, preferred_element_type=jnp.float32)  11 us
  transfers between devices with their start and end apart: 3, of which 2 were waited for; matrix products, arithmetic and copies ran while one was open for 14% of the time, Pallas kernels for 0%

commit v1 on v0

v1 whole, which is shorter than its diff:
```python
import math

import jax
import jax.numpy as jnp
from jax import lax
from jax.experimental import pallas as pl
from jax.experimental.pallas import tpu as pltpu
from jax.sharding import PartitionSpec as P

NBIN = 2048
SEGLEN = 4096
NSEG = 4
BAND = 64
NLAG = 512
SIDE = 4
RADIX = 16
INNER = SEGLEN // RADIX
LANES = 128
HALF_ROWS = 2 * (RADIX // 2)


def split_table(table):
    upper = table.astype(jnp.bfloat16)
    lower = (table - upper.astype(jnp.float32)).astype(jnp.bfloat16)
    return (upper, lower)


def lane_bins():
    lane = jnp.arange(LANES, dtype=jnp.int32)
    return 4 * (lane % 32) + lane // 32


def inner_table():
    times = jnp.arange(INNER, dtype=jnp.int32)
    low = lane_bins()
    high = INNER - 1 - low
    turn = 2.0 * math.pi / INNER

    def block(bins, sign):
        angle = (times[:, None] * bins[None, :] % INNER).astype(jnp.float32) * turn
        cos, sin = jnp.cos(angle), jnp.sin(angle)
        top = jnp.concatenate([cos, -sign * sin], axis=1)
        bottom = jnp.concatenate([sin, sign * cos], axis=1)
        return jnp.concatenate([top, bottom], axis=0)

    return split_table(jnp.concatenate([block(low, 1.0), block(high, -1.0)], axis=1))


def twiddle_table():
    rows = jnp.arange(RADIX, dtype=jnp.int32)
    times = jnp.arange(INNER, dtype=jnp.int32)
    angle = (rows[:, None] * times[None, :] % SEGLEN).astype(jnp.float32) * (2.0 * math.pi / SEGLEN)
    return jnp.stack([jnp.cos(angle), -jnp.sin(angle)], axis=0)


def inverse_table(core):
    row = jnp.arange(NBIN, dtype=jnp.int32)
    part = row // (NBIN // 2)
    outer = core * (RADIX // 2) + row // LANES % (RADIX // 2)
    lane = row % LANES
    bins = outer + RADIX * (4 * (lane % 32) + lane // 32)
    lags = (jnp.arange(NLAG, dtype=jnp.int32) - NLAG // 2) % SEGLEN
    phase = (bins[:, None] * lags[None, :] + part[:, None] * (SEGLEN // 4)) % SEGLEN
    angle = phase.astype(jnp.float32) * (2.0 * math.pi / SEGLEN)
    weight = jnp.where(bins == 0, 1.0, 2.0).astype(jnp.float32) * (0.5 / math.sqrt(NSEG * NBIN))
    return (weight[:, None] * jnp.cos(angle)).astype(jnp.bfloat16)


def real_dft(values):
    n = len(values)
    if n == 2:
        return [(values[0] + values[1], None), (values[0] - values[1], None)]
    even = real_dft(values[0::2])
    odd = real_dft(values[1::2])
    out = [None] * (n // 2 + 1)
    for k in range(n // 4 + 1):
        er, ei = even[k]
        pr, pi = odd[k]
        c, s = math.cos(2 * math.pi * k / n), math.sin(2 * math.pi * k / n)
        if k == 0:
            out[0] = (er + pr, None)
            out[n // 2] = (er - pr, None)
        elif 4 * k == n:
            out[k] = (er, -pr)
        else:
            if 8 * k == n:
                tr, ti = (pr + pi) * c, (pi - pr) * c
            else:
                tr, ti = pr * c + pi * s, pi * c - pr * s
            out[k] = (er + tr, ei + ti)
            out[n // 2 - k] = (er - tr, ti - ei)
    return out


def whiten_kernel(core_ref, x_ref, tw_ref, upper_ref, lower_ref, mine_ref, other_ref, hi_ref, lo_ref, out_ref):
    rows = x_ref.shape[1]
    slices = []
    for t in range(RADIX):
        q, u = t // SIDE, t % SIDE
        slices.append(x_ref[q, :, u * INNER:(u + 1) * INNER].astype(jnp.float32))
    outer = real_dft(slices)
    for f in range(RADIX // 2 + 1):
        re, im = outer[f]
        c, s = tw_ref[0, f:f + 1, :], tw_ref[1, f:f + 1, :]
        if f == 0:
            pair = (re, jnp.zeros_like(re))
        elif im is None:
            pair = (re * c, re * s)
        else:
            pair = (re * c - im * s, re * s + im * c)
        for k in range(2):
            hi = pair[k].astype(jnp.bfloat16)
            hi_ref[f * rows:(f + 1) * rows, k * INNER:(k + 1) * INNER] = hi
            lo_ref[f * rows:(f + 1) * rows, k * INNER:(k + 1) * INNER] = (pair[k] - hi.astype(jnp.float32)).astype(jnp.bfloat16)
    hi, lo = hi_ref[...], lo_ref[...]
    upper, lower = upper_ref[...], lower_ref[...]
    spectrum = jnp.dot(hi, upper, preferred_element_type=jnp.float32)
    spectrum += jnp.dot(hi, lower, preferred_element_type=jnp.float32)
    spectrum += jnp.dot(lo, upper, preferred_element_type=jnp.float32)

    def part(f, k):
        g, base = (f, 0) if f <= RADIX // 2 else (RADIX - f, 2)
        return spectrum[g * rows:(g + 1) * rows, (base + k) * LANES:(base + k + 1) * LANES]

    power = None
    for f in range(RADIX):
        re, im = part(f, 0), part(f, 1)
        both = re * re + im * im
        power = both if power is None else power + both
    power = power + pltpu.roll(power, 64, 1)
    power = power + pltpu.roll(power, 32, 1)
    scale = 1.0 / jnp.sqrt(power * (1.0 / BAND) + 1e-06)
    for f in range(RADIX):
        for k in range(2):
            index = (f // 8) * HALF_ROWS + k * 8 + f % 8
            out_ref[:, index, :] = part(f, k) * scale
    core = core_ref[0]
    mine_ref[...] = out_ref[:, pl.ds(pl.multiple_of(core * HALF_ROWS, HALF_ROWS), HALF_ROWS), :].astype(jnp.bfloat16)
    other_ref[...] = out_ref[:, pl.ds(pl.multiple_of((1 - core) * HALF_ROWS, HALF_ROWS), HALF_ROWS), :].astype(jnp.bfloat16)


def whiten(core, samples, twiddle, upper, lower):
    rows = samples.shape[1]
    out = jax.ShapeDtypeStruct((rows, NSEG * HALF_ROWS, LANES), jnp.bfloat16)
    spec = pl.BlockSpec((rows, HALF_ROWS, LANES), lambda s, c: (0, s, 0))
    count = RADIX // 2 + 1
    return pl.pallas_call(
        whiten_kernel,
        out_shape=(out, out),
        grid_spec=pltpu.PrefetchScalarGridSpec(
            num_scalar_prefetch=1,
            grid=(NSEG,),
            in_specs=[
                pl.BlockSpec((SIDE, rows, SEGLEN // SIDE), lambda s, c: (s, 0, 0)),
                pl.BlockSpec((2, RADIX, INNER), lambda s, c: (0, 0, 0)),
                pl.BlockSpec((2 * INNER, 4 * LANES), lambda s, c: (0, 0)),
                pl.BlockSpec((2 * INNER, 4 * LANES), lambda s, c: (0, 0)),
            ],
            out_specs=(spec, spec),
            scratch_shapes=[
                pltpu.VMEM((count * rows, 2 * INNER), jnp.bfloat16),
                pltpu.VMEM((count * rows, 2 * INNER), jnp.bfloat16),
                pltpu.VMEM((rows, 2 * HALF_ROWS, LANES), jnp.float32),
            ],
        ),
        compiler_params=pltpu.CompilerParams(vmem_limit_bytes=48 << 20),
        name="whiten",
    )(core, samples, twiddle, upper, lower)


def correlate_kernel(src_ref, rcv_ref, sources_ref, mine_ref, sister_ref, table_ref, out_ref, cross_ref):
    chunk = out_ref.shape[0]
    base = pl.program_id(0) * chunk

    def run(receivers_ref):
        def one(i, carry):
            a = sources_ref[src_ref[base + i]].astype(jnp.float32)
            b = receivers_ref[rcv_ref[base + i]].astype(jnp.float32)
            re = im = None
            for s in range(NSEG):
                ar, ai = a[s * 16:s * 16 + 8], a[s * 16 + 8:s * 16 + 16]
                br, bi = b[s * 16:s * 16 + 8], b[s * 16 + 8:s * 16 + 16]
                r = ar * br + ai * bi
                m = ai * br - ar * bi
                re = r if re is None else re + r
                im = m if im is None else im + m
            cross_ref[i, 0:8, :] = re
            cross_ref[i, 8:16, :] = im
            return carry

        lax.fori_loop(0, chunk, one, 0, unroll=8)

    half = pl.num_programs(0) // 2

    @pl.when(pl.program_id(0) < half)
    def _():
        run(mine_ref)

    @pl.when(pl.program_id(0) >= half)
    def _():
        run(sister_ref)

    cross = jnp.concatenate([cross_ref[:, g, :].astype(jnp.bfloat16) for g in range(HALF_ROWS)], axis=1)
    out_ref[...] = jnp.dot(cross, table_ref[...], preferred_element_type=jnp.float32).astype(jnp.bfloat16)


def correlate(source_at, receiver_at, sources, mine, sister, table):
    slots = source_at.shape[0]
    chunk = 128
    whole = lambda a: pl.BlockSpec(a.shape, lambda i, s, r: (0,) * a.ndim)
    return pl.pallas_call(
        correlate_kernel,
        out_shape=jax.ShapeDtypeStruct((slots, NLAG), jnp.bfloat16),
        grid_spec=pltpu.PrefetchScalarGridSpec(
            num_scalar_prefetch=2,
            grid=(slots // chunk,),
            in_specs=[whole(sources), whole(mine), whole(sister), whole(table)],
            out_specs=pl.BlockSpec((chunk, NLAG), lambda i, s, r: (i, 0)),
            scratch_shapes=[pltpu.VMEM((chunk, HALF_ROWS, LANES), jnp.float32)],
        ),
        compiler_params=pltpu.CompilerParams(vmem_limit_bytes=48 << 20),
        name="correlate",
    )(source_at, receiver_at, sources, mine, sister, table)


def shift(value, axis, step):
    if axis == "core":
        return lax.ppermute(value, "gx", [(g, g ^ 1) for g in range(2 * SIDE)])
    if axis == "y":
        return lax.ppermute(value, "gx", [(g, (g + 2 * step) % (2 * SIDE)) for g in range(2 * SIDE)])
    if axis == "z":
        return lax.ppermute(value, "gy", [(g, (g + SIDE * step) % (SIDE * SIDE)) for g in range(SIDE * SIDE)])
    return lax.ppermute(value, "gy", [(g, g // SIDE * SIDE + (g + step) % SIDE) for g in range(SIDE * SIDE)])


def gather_ring(value, axis):
    return jnp.stack([value] + [shift(value, axis, d) for d in (1, 2, 3)], axis=0)


def gather_last(value, axis):
    ahead, behind = shift(value, axis, 1), shift(value, axis, 3)
    n = value.shape[0] // 2
    far = jnp.concatenate([shift(ahead[:n], axis, 1), shift(behind[n:], axis, 3)], axis=0)
    return jnp.stack([value, ahead, far, behind], axis=0)


def body(raw_window, source_ids, pair_source, pair_holder, pair_receiver):
    groups = lax.axis_size("gy")
    devices = lax.axis_size("gx") * groups
    gx, gy = lax.axis_index("gx"), lax.axis_index("gy")
    place = {"core": gx % 2, "y": gx // 2, "z": gy // SIDE, "x": gy % SIDE}
    core = place["core"]
    span = raw_window.shape[1]
    sample = (gy * span + jnp.arange(span, dtype=jnp.int32)) % SEGLEN
    taper = jnp.sin(math.pi * (sample.astype(jnp.float32) + 0.5) / SEGLEN) ** 2
    tapered = (raw_window * taper[None, :]).astype(jnp.bfloat16)
    channels = raw_window.shape[0] // groups
    samples = lax.all_to_all(tapered.reshape(groups, channels, span), "gy", split_axis=0, concat_axis=0, tiled=True)

    pairs = pair_source.shape[0]
    holder = pair_holder[:, 0]
    order = jnp.arange(pairs, dtype=jnp.int32)
    same = (holder[:, None] == holder[None, :]) & (order[None, :] < order[:, None])
    rank = jnp.sum(same.astype(jnp.int32), axis=1)
    slot = holder * 2 + rank
    packed = pair_receiver * 256 + pair_source
    named = jnp.arange(2 * devices, dtype=jnp.int32)[:, None] == slot[None, :]
    outgoing = jnp.sum(jnp.where(named, packed[None, :], 0), axis=1).reshape(devices, 2)
    incoming = lax.all_to_all(outgoing, ("gx", "gy"), split_axis=0, concat_axis=0, tiled=True).reshape(-1)
    asked = jnp.concatenate([incoming, shift(incoming, "core", 1)])
    receiver_at, source_no = asked // 256, asked % 256

    twiddle = twiddle_table()
    upper, lower = inner_table()
    table = inverse_table(core)

    mine, other = whiten(core.reshape(1), samples, twiddle, upper, lower)
    sister = shift(other, "core", 1)
    here = gx * groups + gy
    local = source_ids - here * channels
    own = jnp.take(mine, local, axis=0)
    theirs = shift(jnp.take(other, local, axis=0), "core", 1)
    block = jnp.stack([own, theirs], axis=0)
    axes = ("x", "z", "y")
    block = gather_ring(block, axes[0])
    block = gather_ring(block, axes[1])
    sources = gather_last(block, axes[2]).reshape(devices * 2, NSEG * HALF_ROWS, LANES)

    device_no = source_no // 2
    at = {"y": device_no // (2 * groups), "z": device_no % groups // SIDE, "x": device_no % SIDE}
    core_at = device_no // groups % 2
    source_at = 0
    for axis in reversed(axes):
        source_at = source_at * SIDE + (place[axis] - at[axis]) % SIDE
    source_at = (source_at * 2 + (core_at ^ core)) * 2 + source_no % 2

    partial = correlate(source_at, receiver_at, sources, mine, sister, table)
    outgoing = jnp.transpose(partial.reshape(2, devices, 2, NLAG), (1, 0, 2, 3))
    returned = lax.all_to_all(outgoing, ("gx", "gy"), split_axis=0, concat_axis=0, tiled=True)
    returned = returned.reshape(devices * 4, NLAG)
    holder_core = holder // groups % 2
    row = jnp.arange(4 * devices, dtype=jnp.int32)
    row_dev, row_rel, row_rank = row // 4, row // 2 % 2, row % 2
    row_holder = jnp.where(row_rel == 0, row_dev, row_dev ^ groups)
    pick = (row_holder[None, :] == holder[:, None]) & (row_rank[None, :] == rank[:, None])
    return jnp.dot(pick.astype(jnp.bfloat16), returned, preferred_element_type=jnp.float32)


def solution(mesh):
    return jax.shard_map(
        body,
        mesh=mesh,
        in_specs=(
            P("gx", "gy"),
            P(("gx", "gy")),
            P(("gx", "gy")),
            P(("gx", "gy"), None),
            P(("gx", "gy")),
        ),
        out_specs=P(("gx", "gy"), None),
        check_vma=False,
    )
```

time: 461 us -> 180 us (0.39)
  other arithmetic: 197 us -> 30.5 us
  waiting for transfers between devices: 127 us -> 62.1 us
  local copies, waits for them, and re-layouts: 58.5 us -> 11.9 us
  starting transfers between devices: 15.4 us -> 50.8 us
  matrix products: 24.1 us -> 0.98 us
  Pallas kernels: 0 us -> 20.5 us
  blocking collectives: 18.1 us -> 0 us
  between operations: 13.9 us -> 0.32 us
  loops' own time: 5.44 us -> 0 us
    cos x8 -> x0, other arithmetic: 132 us -> none  [whiten_block(): jnp.cos(angle)]
    all_to_all x2 -> x3, waiting for transfers between devices: 126 us -> 39.1 us  [the longest x1 27 us: body(): lax.all_to_all(tapered.reshape(groups, channels, span), 'gy', split_axis=...]
    gather x4 -> x2, local copies, waits for them, and re-layouts: 35 us -> 3.57 us  [the longest x1 1.78 us: body(): own = jnp.take(mine, local, axis=0)]
    dot_general x18 -> x1, matrix products: 24.1 us -> 0.98 us  [body(): jnp.dot(pick.astype(jnp.bfloat16), returned, preferred_element_type=jnp.f...]
    ppermute x0 -> x13, waiting for transfers between devices: none -> 23 us  [the longest x3 11.6 us: shift(): lax.ppermute(value, 'gy', [(g, (g + SIDE * step) % (SIDE * SIDE)) for g i...]
    pallas_call x0 -> x2, Pallas kernels: none -> 20.5 us  [the longest x1 11.1 us: correlate(): pl.pallas_call(correlate_kernel, out_shape=jax.ShapeDtypeStruct((slots, N...]
    ppermute x0 -> x13, starting transfers between devices: none -> 19 us  [the longest x3 6.07 us: shift(): lax.ppermute(value, 'gy', [(g, g // SIDE * SIDE + (g + step) % SIDE) for...]
    all_to_all x1 -> x0, blocking collectives: 18.1 us -> none  [body(): lax.all_to_all(outgoing, ('gx', 'gy'), split_axis=0, concat_axis=0, tiled...]
  transfers between devices with their start and end apart: 3 -> 16, of which waited for: 2 -> 10; matrix products, arithmetic and copies ran while one was open for 14% -> 15% of each run, Pallas kernels for 0% -> 0%
where the time goes in v1:
time: 180 us; the launch traced here: 177 us
  waiting for transfers between devices  62.1 us (34%)
  starting transfers between devices  50.8 us (28%)
  other arithmetic  30.5 us (17%)
  Pallas kernels  20.5 us (11%)
  local copies, waits for them, and re-layouts  11.9 us (7%)
    all_to_all x1, waiting for transfers between devices, body(): lax.all_to_all(tapered.reshape(groups, channels, span), 'gy', split_axis=...  27 us
    all_to_all x2, starting transfers between devices, body(): lax.all_to_all(outgoing, ('gx', 'gy'), split_axis=0, concat_axis=0, tiled...  24.1 us
    convert_element_type x1, other arithmetic, inverse_table(): return (weight[:, None] * jnp.cos(angle)).astype(jnp.bfloat16)  17.2 us
    all_to_all x2, waiting for transfers between devices, body(): lax.all_to_all(outgoing, ('gx', 'gy'), split_axis=0, concat_axis=0, tiled...  12.1 us
    ppermute x3, waiting for transfers between devices, shift(): lax.ppermute(value, 'gy', [(g, (g + SIDE * step) % (SIDE * SIDE)) for g i...  11.6 us
    pallas_call x1, Pallas kernels, correlate(): pl.pallas_call(correlate_kernel, out_shape=jax.ShapeDtypeStruct((slots, N...  11.1 us
    pallas_call x1, Pallas kernels, whiten(): pl.pallas_call(whiten_kernel, out_shape=(out, out), grid_spec=pltpu.Prefe...  9.4 us
    all_to_all x1, starting transfers between devices, body(): lax.all_to_all(tapered.reshape(groups, channels, span), 'gy', split_axis=...  7.73 us
  transfers between devices with their start and end apart: 16, of which 10 were waited for; matrix products, arithmetic and copies ran while one was open for 15% of the time, Pallas kernels for 0%

profile of v1, /device:TPU:5, one launch (start us, length us, event | category | flops | bytes accessed | tf_op | source)
XLA Modules:
  0.0 177.2 jit_solution(17905249176455754015)
XLA Ops:
  0.1 4.1 %multiply_convert_fusion = bf16[1024,1024]{1,0:T(8,128)(2,1)} fusion(f32[1024,1024]{1,0:T(8,128)} %param.7, f32[1024]{0:T(1024)S(1)} %fusion.71), kind=kLoop, calls=%fused_computation.12 | loop fusion | flops 2097152 | bytes 6295552 | tf_op jit(solution)/shard_map/convert_element_type | solution.py:256
  4.2 7.7 %all-to-all-start.1 = ((bf16[16,64,1024]{2,1,0:T(8,128)(2,1)}), bf16[16,64,1024]{2,1,0:T(8,128)(2,1)S(1)}, u32[]{:S(2)}, u32[]{:S(2)}) async-start(bf16[16,64,1024]{2,1,0:T(8,128)(2,1)} %bitcast.30), calls=%async_computation.1 | async-start | bytes 4194304 | tf_op jit(solution)/shard_map/all_to_all | solution.py:258
  12.1 1.0 broadcast_multiply_fusion.1
  13.3 27.0 %all-to-all-done.1.x_ref = bf16[16,64,1024]{2,1,0:T(8,128)(2,1)S(1)} async-done(((bf16[16,64,1024]{2,1,0:T(8,128)(2,1)}), bf16[16,64,1024]{2,1,0:T(8,128)(2,1)S(1)}, u32[]{:S(2)}, u32[]{:S(2)}) %all-to-all-start.1) | async-done | bytes 2097184 | tf_op jit(solution)/shard_map/all_to_all | solution.py:258
  40.4 9.4 %whiten.1 = (bf16[64,64,128]{2,1,0:T(8,128)(2,1)S(1)}, bf16[64,64,128]{2,1,0:T(8,128)(2,1)}) custom-call(s32[1]{0:T(128)} %bitcast.2.core_ref, bf16[16,64,1024]{2,1,0:T(8,128)(2,1)S(1)} %all-to-all-done.1.x_ref, f32[2,16,256]{2,1,0:T(8,128)S(1)} %pad_maximum_fusion.4.tw_ref, bf16[512,512]{1,0:T(8,128)(2,1)S(1)} %fusion.10.upper_ref, ...), custom_call_target="tpu_custom_call" | custom-call | tf_op jit(solution)/shard_map/whiten/pallas_call | solution.py:147
  49.8 1.0 copy-done
  50.8 1.8 %gather_fusion.1 = bf16[2,64,128]{2,1,0:T(8,128)(2,1)S(1)} fusion(bf16[64,64,128]{2,1,0:T(8,128)(2,1)} %get-tuple-element.9, s32[1024]{0:T(1024)S(1)} %pad_clamp_fusion), kind=kCustom, calls=%fused_computation.1.clone | custom fusion | bytes 65544 | tf_op jit(solution)/shard_map/jit(_take)/gather | solution.py:282
  52.6 1.8 %gather_fusion = bf16[2,64,128]{2,1,0:T(8,128)(2,1)S(1)} fusion(bf16[64,64,128]{2,1,0:T(8,128)(2,1)} %copy-done, s32[1024]{0:T(1024)S(1)} %pad_clamp_fusion), kind=kCustom, calls=%fused_computation.clone | custom fusion | bytes 65544 | tf_op jit(solution)/shard_map/jit(_take)/gather | solution.py:281
  55.8 1.7 collective-permute-start.2
  57.5 2.4 %collective-permute-start.3 = (bf16[2,2,64,128]{3,2,1,0:T(8,128)(2,1)S(1)}, bf16[2,2,64,128]{3,2,1,0:T(8,128)(2,1)S(1)}, u32[]{:S(2)}, u32[]{:S(2)}) collective-permute-start(bf16[2,2,64,128]{3,2,1,0:T(8,128)(2,1)S(1)} %get-tuple-element.17), channel_id=1, source_target_pairs={{0,2},{1,3},{2,0},{3,1},{4,6},{5,7},{6,4},{7,5},{8,10},{9,11},{10,... | collective-permute-start | bytes 196616 | tf_op jit(solution)/shard_map/ppermute | solution.py:233
  59.9 2.0 %collective-permute-start.4 = (bf16[2,2,64,128]{3,2,1,0:T(8,128)(2,1)S(1)}, bf16[2,2,64,128]{3,2,1,0:T(8,128)(2,1)S(1)}, u32[]{:S(2)}, u32[]{:S(2)}) collective-permute-start(bf16[2,2,64,128]{3,2,1,0:T(8,128)(2,1)S(1)} %get-tuple-element.17), channel_id=1, source_target_pairs={{0,3},{1,0},{2,1},{3,2},{4,7},{5,4},{6,5},{7,6},{8,11},{9,8},{10,9... | collective-permute-start | bytes 196616 | tf_op jit(solution)/shard_map/ppermute | solution.py:233
  61.9 1.4 collective-permute-done.3
  64.3 2.3 %collective-permute-start.6 = (bf16[4,2,2,64,128]{4,3,2,1,0:T(8,128)(2,1)S(1)}, bf16[4,2,2,64,128]{4,3,2,1,0:T(8,128)(2,1)S(1)}, u32[]{:S(2)}, u32[]{:S(2)}) collective-permute-start(bf16[4,2,2,64,128]{4,3,2,1,0:T(8,128)(2,1)S(1)} %get-tuple-element.15), channel_id=1, source_target_pairs={{0,8},{1,9},{2,10},{3,11},{4,12},{5,13},{6,14},{7,15},{8,0},{9,1},... | collective-permute-start | bytes 786440 | tf_op jit(solution)/shard_map/ppermute | solution.py:232
  67.0 4.9 %collective-permute-done.5 = bf16[4,2,2,64,128]{4,3,2,1,0:T(8,128)(2,1)S(1)} collective-permute-done((bf16[4,2,2,64,128]{4,3,2,1,0:T(8,128)(2,1)S(1)}, bf16[4,2,2,64,128]{4,3,2,1,0:T(8,128)(2,1)S(1)}, u32[]{:S(2)}, u32[]{:S(2)}) %collective-permute-start.5) | collective-permute-done | bytes 262176 | tf_op jit(solution)/shard_map/ppermute | solution.py:232
  71.8 5.5 %collective-permute-done.6 = bf16[4,2,2,64,128]{4,3,2,1,0:T(8,128)(2,1)S(1)} collective-permute-done((bf16[4,2,2,64,128]{4,3,2,1,0:T(8,128)(2,1)S(1)}, bf16[4,2,2,64,128]{4,3,2,1,0:T(8,128)(2,1)S(1)}, u32[]{:S(2)}, u32[]{:S(2)}) %collective-permute-start.6) | collective-permute-done | bytes 262176 | tf_op jit(solution)/shard_map/ppermute | solution.py:232
  77.4 1.2 collective-permute-done.7
  78.6 1.5 fusion.108
  80.1 2.7 %collective-permute-start.10 = (bf16[4,4,2,2,64,128]{5,4,3,2,1,0:T(8,128)(2,1)}, bf16[4,4,2,2,64,128]{5,4,3,2,1,0:T(8,128)(2,1)S(1)}, u32[]{:S(2)}, u32[]{:S(2)}) collective-permute-start(bf16[4,4,2,2,64,128]{5,4,3,2,1,0:T(8,128)(2,1)} %get-tuple-element.13), channel_id=1, source_target_pairs={{0,96},{16,112},{32,0},{48,16},{64,32},{80,48},{96,64},{112,80},{1... | collective-permute-start | bytes 3145736 | tf_op jit(solution)/shard_map/ppermute | solution.py:230
  83.9 12.4 %all-to-all-start = ((s32[128,1,2]{2,1,0:T(1,128)}), s32[128,1,2]{2,1,0:T(1,128)S(1)}, u32[]{:S(2)}, u32[]{:S(2)}) async-start(s32[128,1,2]{2,1,0:T(1,128)} %bitcast.1), calls=%async_computation | async-start | bytes 131072 | tf_op jit(solution)/shard_map/all_to_all | solution.py:269
  96.9 7.7 %collective-permute-done.10 = bf16[4,4,2,2,64,128]{5,4,3,2,1,0:T(8,128)(2,1)S(1)} collective-permute-done((bf16[4,4,2,2,64,128]{5,4,3,2,1,0:T(8,128)(2,1)}, bf16[4,4,2,2,64,128]{5,4,3,2,1,0:T(8,128)(2,1)S(1)}, u32[]{:S(2)}, u32[]{:S(2)}) %collective-permute-start.10) | collective-permute-done | bytes 1048608 | tf_op jit(solution)/shard_map/ppermute | solution.py:230
  105.5 3.3 %collective-permute-start.11 = (bf16[2,4,2,2,64,128]{5,4,3,2,1,0:T(8,128)(2,1)}, bf16[2,4,2,2,64,128]{5,4,3,2,1,0:T(8,128)(2,1)}, u32[]{:S(2)}, u32[]{:S(2)}) collective-permute-start(bf16[2,4,2,2,64,128]{5,4,3,2,1,0:T(8,128)(2,1)} %slice.13), channel_id=1, source_target_pairs={{0,96},{16,112},{32,0},{48,16},{64,32},{80,48},{96,64},{112,80},{1... | collective-permute-start | bytes 1572872 | tf_op jit(solution)/shard_map/ppermute | solution.py:230
  110.0 17.2 %fusion.5.table_ref = bf16[2048,512]{1,0:T(8,128)(2,1)S(1)} fusion(s32[2048]{0:T(1024)S(1)} %get-tuple-element.36, s32[512]{0:T(512)S(1)} %add_select_fusion.10, s32[2048]{0:T(1024)S(1)} %get-tuple-element.35, f32[2048]{0:T(1024)S(1)} %select_multiply_fusion), kind=kLoop, calls=%fused_computation.10 | loop fusion | flops 17825792 | bytes 2123776 | tf_op jit(solution)/shard_map/convert_element_type | solution.py:66
  128.7 2.9 %collective-permute-start = (s32[256]{0:T(256)S(1)}, s32[256]{0:T(256)S(1)}, u32[]{:S(2)}, u32[]{:S(2)}) collective-permute-start(s32[256]{0:T(256)S(1)} %reshape.294), channel_id=1, source_target_pairs={{0,16},{16,0},{32,48},{48,32},{64,80},{80,64},{96,112},{112,96},{1... | collective-permute-start | bytes 3080 | tf_op jit(solution)/shard_map/ppermute | solution.py:228
  132.6 1.3 maximum_bitcast_fusion
  133.9 3.7 %pad_maximum_fusion = bf16[4,4,4,2,2,64,128]{6,5,4,3,2,1,0:T(8,128)(2,1)} fusion(bf16[1,4,4,2,2,64,128]{6,5,4,3,2,1,0:T(8,128)(2,1)} %bitcast.31, bf16[1,4,4,2,2,64,128]{6,5,4,3,2,1,0:T(8,128)(2,1)S(1)} %maximum_bitcast_fusion, bf16[1,4,4,2,2,64,128]{6,5,4,3,2,1,0:T(8,128)(2,1)} %bitcast.32, bf16[1,4,4,2,2,64,128]{6,5,4,3,2,1,0:T(8,128)(2,1)} %get-tuple-element.12), kind=kLoop, calls=%fused_computation.11 | loop fusion | flops 6291456 | bytes 8388608 | tf_op jit(solution)/shard_map/stack | solution.py:244
  137.6 1.0 copy-done.2
  138.6 1.2 copy-done.3
  139.8 11.1 %correlate.1 = bf16[512,512]{1,0:T(8,128)(2,1)S(1)} custom-call(s32[512]{0:T(512)S(1)} %get-tuple-element.19.src_ref, s32[512]{0:T(512)S(1)} %get-tuple-element.18.rcv_ref, bf16[256,64,128]{2,1,0:T(8,128)(2,1)} %bitcast.29, bf16[64,64,128]{2,1,0:T(8,128)(2,1)S(1)} %copy-done.1, bf16[64,64,128]{2,1,0:T(8,128)(2,1)S(1)} %copy-done.3, ...), custom_call_target="tpu_custom_call" | custom-call | tf_op jit(solution)/shard_map/correlate/pallas_call | solution.py:211
  151.2 1.2 copy.12
  152.3 11.6 %all-to-all-start.2 = ((bf16[128,2,2,512]{3,2,1,0:T(2,128)(2,1)}), bf16[128,2,2,512]{3,2,1,0:T(2,128)(2,1)S(1)}, u32[]{:S(2)}, u32[]{:S(2)}) async-start(bf16[128,2,2,512]{3,2,1,0:T(2,128)(2,1)} %bitcast.28), calls=%async_computation.2 | async-start | bytes 1048576 | tf_op jit(solution)/shard_map/all_to_all | solution.py:299
  164.0 12.1 %all-to-all-done.2 = bf16[128,2,2,512]{3,2,1,0:T(2,128)(2,1)S(1)} async-done(((bf16[128,2,2,512]{3,2,1,0:T(2,128)(2,1)}), bf16[128,2,2,512]{3,2,1,0:T(2,128)(2,1)S(1)}, u32[]{:S(2)}, u32[]{:S(2)}) %all-to-all-start.2) | async-done | bytes 524320 | tf_op jit(solution)/shard_map/all_to_all | solution.py:299
  176.2 1.0 fusion.6
  (63 shorter events, 9.5 us)
Async XLA Ops:
  0.1 11.9 %copy-start.7 = (s32[2]{0:T(128)S(1)}, s32[2]{0:T(128)}, u32[]{:S(2)}) copy-start(s32[2]{0:T(128)} %param.8) | copy-start | bytes 28
  4.2 36.1 %all-to-all-start.1 = ((bf16[16,64,1024]{2,1,0:T(8,128)(2,1)}), bf16[16,64,1024]{2,1,0:T(8,128)(2,1)S(1)}, u32[]{:S(2)}, u32[]{:S(2)}) async-start(bf16[16,64,1024]{2,1,0:T(8,128)(2,1)} %bitcast.30), calls=%async_computation.1 | async-start | bytes 4194304 | tf_op jit(solution)/shard_map/all_to_all | solution.py:258
  13.2 69.6 %copy-start.6 = (s32[128,1]{0,1:T(1,128)S(1)}, s32[128,1]{0,1:T(1,128)}, u32[]{:S(2)}) copy-start(s32[128,1]{0,1:T(1,128)} %param.10) | copy-start | bytes 1540
  13.2 69.8 %copy-start.8 = (s32[128]{0:T(128)S(1)}, s32[128]{0:T(128)}, u32[]{:S(2)}) copy-start(s32[128]{0:T(128)} %param.9) | copy-start | bytes 1540
  13.2 69.8 %copy-start.9 = (s32[128]{0:T(128)S(1)}, s32[128]{0:T(128)}, u32[]{:S(2)}) copy-start(s32[128]{0:T(128)} %param.11) | copy-start | bytes 1540
  49.8 1.0 copy-start
  54.4 1.4 collective-permute-start.1
  55.8 6.1 %collective-permute-start.2 = (bf16[2,2,64,128]{3,2,1,0:T(8,128)(2,1)S(1)}, bf16[2,2,64,128]{3,2,1,0:T(8,128)(2,1)S(1)}, u32[]{:S(2)}, u32[]{:S(2)}) collective-permute-start(bf16[2,2,64,128]{3,2,1,0:T(8,128)(2,1)S(1)} %get-tuple-element.17), channel_id=1, source_target_pairs={{0,1},{1,2},{2,3},{3,0},{4,5},{5,6},{6,7},{7,4},{8,9},{9,10},{10,1... | collective-permute-start | bytes 196616 | tf_op jit(solution)/shard_map/ppermute | solution.py:233
  57.5 5.8 %collective-permute-start.3 = (bf16[2,2,64,128]{3,2,1,0:T(8,128)(2,1)S(1)}, bf16[2,2,64,128]{3,2,1,0:T(8,128)(2,1)S(1)}, u32[]{:S(2)}, u32[]{:S(2)}) collective-permute-start(bf16[2,2,64,128]{3,2,1,0:T(8,128)(2,1)S(1)} %get-tuple-element.17), channel_id=1, source_target_pairs={{0,2},{1,3},{2,0},{3,1},{4,6},{5,7},{6,4},{7,5},{8,10},{9,11},{10,... | collective-permute-start | bytes 196616 | tf_op jit(solution)/shard_map/ppermute | solution.py:233
  59.9 4.0 %collective-permute-start.4 = (bf16[2,2,64,128]{3,2,1,0:T(8,128)(2,1)S(1)}, bf16[2,2,64,128]{3,2,1,0:T(8,128)(2,1)S(1)}, u32[]{:S(2)}, u32[]{:S(2)}) collective-permute-start(bf16[2,2,64,128]{3,2,1,0:T(8,128)(2,1)S(1)} %get-tuple-element.17), channel_id=1, source_target_pairs={{0,3},{1,0},{2,1},{3,2},{4,7},{5,4},{6,5},{7,6},{8,11},{9,8},{10,9... | collective-permute-start | bytes 196616 | tf_op jit(solution)/shard_map/ppermute | solution.py:233
  63.9 7.9 %collective-permute-start.5 = (bf16[4,2,2,64,128]{4,3,2,1,0:T(8,128)(2,1)S(1)}, bf16[4,2,2,64,128]{4,3,2,1,0:T(8,128)(2,1)S(1)}, u32[]{:S(2)}, u32[]{:S(2)}) collective-permute-start(bf16[4,2,2,64,128]{4,3,2,1,0:T(8,128)(2,1)S(1)} %get-tuple-element.15), channel_id=1, source_target_pairs={{0,4},{1,5},{2,6},{3,7},{4,8},{5,9},{6,10},{7,11},{8,12},{9,13},{1... | collective-permute-start | bytes 786440 | tf_op jit(solution)/shard_map/ppermute | solution.py:232
  64.3 13.0 %collective-permute-start.6 = (bf16[4,2,2,64,128]{4,3,2,1,0:T(8,128)(2,1)S(1)}, bf16[4,2,2,64,128]{4,3,2,1,0:T(8,128)(2,1)S(1)}, u32[]{:S(2)}, u32[]{:S(2)}) collective-permute-start(bf16[4,2,2,64,128]{4,3,2,1,0:T(8,128)(2,1)S(1)} %get-tuple-element.15), channel_id=1, source_target_pairs={{0,8},{1,9},{2,10},{3,11},{4,12},{5,13},{6,14},{7,15},{8,0},{9,1},... | collective-permute-start | bytes 786440 | tf_op jit(solution)/shard_map/ppermute | solution.py:232
  66.6 12.0 %collective-permute-start.7 = (bf16[4,2,2,64,128]{4,3,2,1,0:T(8,128)(2,1)S(1)}, bf16[4,2,2,64,128]{4,3,2,1,0:T(8,128)(2,1)S(1)}, u32[]{:S(2)}, u32[]{:S(2)}) collective-permute-start(bf16[4,2,2,64,128]{4,3,2,1,0:T(8,128)(2,1)S(1)} %get-tuple-element.15), channel_id=1, source_target_pairs={{0,12},{1,13},{2,14},{3,15},{4,0},{5,1},{6,2},{7,3},{8,4},{9,5},{1... | collective-permute-start | bytes 786440 | tf_op jit(solution)/shard_map/ppermute | solution.py:232
  80.1 24.5 %collective-permute-start.10 = (bf16[4,4,2,2,64,128]{5,4,3,2,1,0:T(8,128)(2,1)}, bf16[4,4,2,2,64,128]{5,4,3,2,1,0:T(8,128)(2,1)S(1)}, u32[]{:S(2)}, u32[]{:S(2)}) collective-permute-start(bf16[4,4,2,2,64,128]{5,4,3,2,1,0:T(8,128)(2,1)} %get-tuple-element.13), channel_id=1, source_target_pairs={{0,96},{16,112},{32,0},{48,16},{64,32},{80,48},{96,64},{112,80},{1... | collective-permute-start | bytes 3145736 | tf_op jit(solution)/shard_map/ppermute | solution.py:230
  82.8 26.0 %collective-permute-start.8 = (bf16[4,4,2,2,64,128]{5,4,3,2,1,0:T(8,128)(2,1)}, bf16[4,4,2,2,64,128]{5,4,3,2,1,0:T(8,128)(2,1)S(1)}, u32[]{:S(2)}, u32[]{:S(2)}) collective-permute-start(bf16[4,4,2,2,64,128]{5,4,3,2,1,0:T(8,128)(2,1)} %get-tuple-element.13), channel_id=1, source_target_pairs={{0,32},{16,48},{32,64},{48,80},{64,96},{80,112},{96,0},{112,16},{1... | collective-permute-start | bytes 3145736 | tf_op jit(solution)/shard_map/ppermute | solution.py:230
  83.9 43.3 %all-to-all-start = ((s32[128,1,2]{2,1,0:T(1,128)}), s32[128,1,2]{2,1,0:T(1,128)S(1)}, u32[]{:S(2)}, u32[]{:S(2)}) async-start(s32[128,1,2]{2,1,0:T(1,128)} %bitcast.1), calls=%async_computation | async-start | bytes 131072 | tf_op jit(solution)/shard_map/all_to_all | solution.py:269
  96.4 41.2 %collective-permute-start.12 = (bf16[64,64,128]{2,1,0:T(8,128)(2,1)}, bf16[64,64,128]{2,1,0:T(8,128)(2,1)S(1)}, u32[]{:S(2)}, u32[]{:S(2)}) collective-permute-start(bf16[64,64,128]{2,1,0:T(8,128)(2,1)} %get-tuple-element.9), channel_id=1, source_target_pairs={{0,16},{16,0},{32,48},{48,32},{64,80},{80,64},{96,112},{112,96},{1... | collective-permute-start | bytes 3145736 | tf_op jit(solution)/shard_map/ppermute | solution.py:228
  104.6 5.1 %copy-start.4 = (bf16[4,4,2,2,64,128]{5,4,3,2,1,0:T(8,128)(2,1)}, bf16[4,4,2,2,64,128]{5,4,3,2,1,0:T(8,128)(2,1)S(1)}, u32[]{:S(2)}) copy-start(bf16[4,4,2,2,64,128]{5,4,3,2,1,0:T(8,128)(2,1)S(1)} %collective-permute-done.10) | copy-start | bytes 3145732
  105.5 27.0 %collective-permute-start.11 = (bf16[2,4,2,2,64,128]{5,4,3,2,1,0:T(8,128)(2,1)}, bf16[2,4,2,2,64,128]{5,4,3,2,1,0:T(8,128)(2,1)}, u32[]{:S(2)}, u32[]{:S(2)}) collective-permute-start(bf16[2,4,2,2,64,128]{5,4,3,2,1,0:T(8,128)(2,1)} %slice.13), channel_id=1, source_target_pairs={{0,96},{16,112},{32,0},{48,16},{64,32},{80,48},{96,64},{112,80},{1... | collective-permute-start | bytes 1572872 | tf_op jit(solution)/shard_map/ppermute | solution.py:230
  108.8 1.2 copy-start.5
  109.7 22.8 %collective-permute-start.9 = (bf16[2,4,2,2,64,128]{5,4,3,2,1,0:T(8,128)(2,1)}, bf16[2,4,2,2,64,128]{5,4,3,2,1,0:T(8,128)(2,1)}, u32[]{:S(2)}, u32[]{:S(2)}) collective-permute-start(bf16[2,4,2,2,64,128]{5,4,3,2,1,0:T(8,128)(2,1)} %slice.12), channel_id=1, source_target_pairs={{0,32},{16,48},{32,64},{48,80},{64,96},{80,112},{96,0},{112,16},{1... | collective-permute-start | bytes 1572872 | tf_op jit(solution)/shard_map/ppermute | solution.py:230
  128.7 3.7 %collective-permute-start = (s32[256]{0:T(256)S(1)}, s32[256]{0:T(256)S(1)}, u32[]{:S(2)}, u32[]{:S(2)}) collective-permute-start(s32[256]{0:T(256)S(1)} %reshape.294), channel_id=1, source_target_pairs={{0,16},{16,0},{32,48},{48,32},{64,80},{80,64},{96,112},{112,96},{1... | collective-permute-start | bytes 3080 | tf_op jit(solution)/shard_map/ppermute | solution.py:228
  133.9 4.7 %copy-start.1 = (bf16[64,64,128]{2,1,0:T(8,128)(2,1)S(1)}, bf16[64,64,128]{2,1,0:T(8,128)(2,1)}, u32[]{:S(2)}) copy-start(bf16[64,64,128]{2,1,0:T(8,128)(2,1)} %copy-done) | copy-start | bytes 3145732
  137.6 1.0 copy-start.2
  138.6 1.2 copy-start.3
  152.3 23.7 %all-to-all-start.2 = ((bf16[128,2,2,512]{3,2,1,0:T(2,128)(2,1)}), bf16[128,2,2,512]{3,2,1,0:T(2,128)(2,1)S(1)}, u32[]{:S(2)}, u32[]{:S(2)}) async-start(bf16[128,2,2,512]{3,2,1,0:T(2,128)(2,1)} %bitcast.28), calls=%async_computation.2 | async-start | bytes 1048576 | tf_op jit(solution)/shard_map/all_to_all | solution.py:299

commit v2 on v1

--- a/solution.py
+++ b/solution.py
@@ -53,17 +53,21 @@
     return jnp.stack([jnp.cos(angle), -jnp.sin(angle)], axis=0)
 
 
+def turns(count, lags):
+    angle = (count[:, None] * lags[None, :] % SEGLEN).astype(jnp.float32) * (2.0 * math.pi / SEGLEN)
+    return jnp.cos(angle), jnp.sin(angle)
+
+
 def inverse_table(core):
-    row = jnp.arange(NBIN, dtype=jnp.int32)
-    part = row // (NBIN // 2)
-    outer = core * (RADIX // 2) + row // LANES % (RADIX // 2)
-    lane = row % LANES
-    bins = outer + RADIX * (4 * (lane % 32) + lane // 32)
+    outer = core * (RADIX // 2) + jnp.arange(RADIX // 2, dtype=jnp.int32)
+    inner = RADIX * lane_bins()
     lags = (jnp.arange(NLAG, dtype=jnp.int32) - NLAG // 2) % SEGLEN
-    phase = (bins[:, None] * lags[None, :] + part[:, None] * (SEGLEN // 4)) % SEGLEN
-    angle = phase.astype(jnp.float32) * (2.0 * math.pi / SEGLEN)
+    (c1, s1), (c2, s2) = lax.optimization_barrier((turns(outer, lags), turns(inner, lags)))
+    c1, s1, c2, s2 = c1[:, None], s1[:, None], c2[None], s2[None]
+    bins = outer[:, None, None] + inner[None, :, None]
     weight = jnp.where(bins == 0, 1.0, 2.0).astype(jnp.float32) * (0.5 / math.sqrt(NSEG * NBIN))
-    return (weight[:, None] * jnp.cos(angle)).astype(jnp.bfloat16)
+    table = jnp.stack([weight * (c1 * c2 - s1 * s2), -weight * (s1 * c2 + c1 * s2)], axis=0)
+    return table.astype(jnp.bfloat16).reshape(NBIN, NLAG)
 
 
 def real_dft(values):
@@ -168,14 +172,31 @@
     )(core, samples, twiddle, upper, lower)
 
 
-def correlate_kernel(src_ref, rcv_ref, sources_ref, mine_ref, sister_ref, table_ref, out_ref, cross_ref):
-    chunk = out_ref.shape[0]
-    base = pl.program_id(0) * chunk
-
-    def run(receivers_ref):
-        def one(i, carry):
-            a = sources_ref[src_ref[base + i]].astype(jnp.float32)
-            b = receivers_ref[rcv_ref[base + i]].astype(jnp.float32)
+GROUP = 8
+
+
+def correlate_kernel(count_ref, src_ref, rcv_ref, slot_ref, *refs):
+    pieces = refs[:-6]
+    table_ref, out_ref, sources_ref, receivers_ref, cross_ref, sems = refs[-6:]
+    copies = []
+    at = {0: 0, 1: 0}
+    for n, piece in enumerate(pieces):
+        which = 1 if n >= len(pieces) - 2 else 0
+        target = receivers_ref if which else sources_ref
+        rows = piece.shape[0]
+        copies.append(pltpu.make_async_copy(piece, target.at[at[which]:at[which] + rows], sems.at[n]))
+        at[which] += rows
+    for copy in copies:
+        copy.start()
+    cross_ref[...] = jnp.zeros_like(cross_ref)
+    for copy in copies:
+        copy.wait()
+
+    def group(g, carry):
+        for u in range(GROUP):
+            i = g * GROUP + u
+            a = sources_ref[src_ref[i]].astype(jnp.float32)
+            b = receivers_ref[rcv_ref[i]].astype(jnp.float32)
             re = im = None
             for s in range(NSEG):
                 ar, ai = a[s * 16:s * 16 + 8], a[s * 16 + 8:s * 16 + 16]
@@ -184,43 +205,46 @@
                 m = ai * br - ar * bi
                 re = r if re is None else re + r
                 im = m if im is None else im + m
-            cross_ref[i, 0:8, :] = re
-            cross_ref[i, 8:16, :] = im
-            return carry
-
-        lax.fori_loop(0, chunk, one, 0, unroll=8)
-
-    half = pl.num_programs(0) // 2
-
-    @pl.when(pl.program_id(0) < half)
-    def _():
-        run(mine_ref)
-
-    @pl.when(pl.program_id(0) >= half)
-    def _():
-        run(sister_ref)
-
-    cross = jnp.concatenate([cross_ref[:, g, :].astype(jnp.bfloat16) for g in range(HALF_ROWS)], axis=1)
-    out_ref[...] = jnp.dot(cross, table_ref[...], preferred_element_type=jnp.float32).astype(jnp.bfloat16)
-
-
-def correlate(source_at, receiver_at, sources, mine, sister, table):
-    slots = source_at.shape[0]
+            slot = slot_ref[i]
+            cross_ref[slot, 0:8, :] = re
+            cross_ref[slot, 8:16, :] = im
+        return carry
+
+    lax.fori_loop(0, (count_ref[0] + GROUP - 1) // GROUP, group, 0)
+    slots = out_ref.shape[0]
     chunk = 128
-    whole = lambda a: pl.BlockSpec(a.shape, lambda i, s, r: (0,) * a.ndim)
+    for c in range(slots // chunk):
+        cross = jnp.concatenate(
+            [cross_ref[c * chunk:(c + 1) * chunk, g, :].astype(jnp.bfloat16) for g in range(HALF_ROWS)], axis=1
+        )
+        product = jnp.dot(cross, table_ref[...], preferred_element_type=jnp.float32)
+        out_ref[c * chunk:(c + 1) * chunk, :] = product.astype(jnp.bfloat16)
+
+
+def correlate(count, source_at, receiver_at, slot_at, pieces, table):
+    slots = slot_at.shape[0]
+    any_spec = pl.BlockSpec(memory_space=pl.ANY)
+    row = pieces[0].shape[1:]
+    n_src = sum(p.shape[0] for p in pieces[:-2])
+    n_rcv = sum(p.shape[0] for p in pieces[-2:])
     return pl.pallas_call(
         correlate_kernel,
         out_shape=jax.ShapeDtypeStruct((slots, NLAG), jnp.bfloat16),
         grid_spec=pltpu.PrefetchScalarGridSpec(
-            num_scalar_prefetch=2,
-            grid=(slots // chunk,),
-            in_specs=[whole(sources), whole(mine), whole(sister), whole(table)],
-            out_specs=pl.BlockSpec((chunk, NLAG), lambda i, s, r: (i, 0)),
-            scratch_shapes=[pltpu.VMEM((chunk, HALF_ROWS, LANES), jnp.float32)],
+            num_scalar_prefetch=4,
+            grid=(1,),
+            in_specs=[any_spec] * len(pieces) + [pl.BlockSpec(table.shape, lambda *_: (0, 0))],
+            out_specs=pl.BlockSpec((slots, NLAG), lambda *_: (0, 0)),
+            scratch_shapes=[
+                pltpu.VMEM((n_src,) + row, jnp.bfloat16),
+                pltpu.VMEM((n_rcv,) + row, jnp.bfloat16),
+                pltpu.VMEM((slots + GROUP, HALF_ROWS, LANES), jnp.float32),
+                pltpu.SemaphoreType.DMA((len(pieces),)),
+            ],
         ),
         compiler_params=pltpu.CompilerParams(vmem_limit_bytes=48 << 20),
         name="correlate",
-    )(source_at, receiver_at, sources, mine, sister, table)
+    )(count, source_at, receiver_at, slot_at, *pieces, table)
 
 
 def shift(value, axis, step):
@@ -237,68 +261,89 @@
     return jnp.stack([value] + [shift(value, axis, d) for d in (1, 2, 3)], axis=0)
 
 
-def gather_last(value, axis):
-    ahead, behind = shift(value, axis, 1), shift(value, axis, 3)
-    n = value.shape[0] // 2
-    far = jnp.concatenate([shift(ahead[:n], axis, 1), shift(behind[n:], axis, 3)], axis=0)
-    return jnp.stack([value, ahead, far, behind], axis=0)
-
-
 def body(raw_window, source_ids, pair_source, pair_holder, pair_receiver):
     groups = lax.axis_size("gy")
     devices = lax.axis_size("gx") * groups
     gx, gy = lax.axis_index("gx"), lax.axis_index("gy")
     place = {"core": gx % 2, "y": gx // 2, "z": gy // SIDE, "x": gy % SIDE}
     core = place["core"]
+    here = gx * groups + gy
     span = raw_window.shape[1]
+    channels = raw_window.shape[0] // groups
     sample = (gy * span + jnp.arange(span, dtype=jnp.int32)) % SEGLEN
     taper = jnp.sin(math.pi * (sample.astype(jnp.float32) + 0.5) / SEGLEN) ** 2
-    tapered = (raw_window * taper[None, :]).astype(jnp.bfloat16)
-    channels = raw_window.shape[0] // groups
-    samples = lax.all_to_all(tapered.reshape(groups, channels, span), "gy", split_axis=0, concat_axis=0, tiled=True)
 
     pairs = pair_source.shape[0]
     holder = pair_holder[:, 0]
     order = jnp.arange(pairs, dtype=jnp.int32)
     same = (holder[:, None] == holder[None, :]) & (order[None, :] < order[:, None])
     rank = jnp.sum(same.astype(jnp.int32), axis=1)
-    slot = holder * 2 + rank
-    packed = pair_receiver * 256 + pair_source
-    named = jnp.arange(2 * devices, dtype=jnp.int32)[:, None] == slot[None, :]
-    outgoing = jnp.sum(jnp.where(named, packed[None, :], 0), axis=1).reshape(devices, 2)
-    incoming = lax.all_to_all(outgoing, ("gx", "gy"), split_axis=0, concat_axis=0, tiled=True).reshape(-1)
-    asked = jnp.concatenate([incoming, shift(incoming, "core", 1)])
-    receiver_at, source_no = asked // 256, asked % 256
+    packed = ((holder * 2 + rank) * channels + pair_receiver) * 256 + pair_source
+    with jax.named_scope("ids"):
+        ids = gather_ring(gather_ring(source_ids - gx * groups * channels, "x"), "z")
+    with jax.named_scope("requests"):
+        notes = gather_ring(gather_ring(packed, "x"), "z")
+        notes = gather_ring(notes, "y")
+        notes = jnp.stack([notes, shift(notes, "core", 1)], axis=0).reshape(devices, pairs)
+
+    per = source_ids.shape[0]
+    step = jnp.arange(groups, dtype=jnp.int32)
+    mate = (place["z"] - step // SIDE) % SIDE * SIDE + (place["x"] - step % SIDE) % SIDE
+    place_of = jnp.sum(jnp.where(mate[None, :] == step[:, None], step[None, :], 0), axis=1)
+    wanted = (ids.reshape(groups, per)[place_of]).reshape(-1)
+    with jax.named_scope("early"):
+        first = (jnp.take(raw_window, wanted, axis=0) * taper[None, :]).astype(jnp.bfloat16)
+        first = jnp.broadcast_to(first[None], (groups,) + first.shape)
+        first = lax.all_to_all(first, "gy", split_axis=0, concat_axis=0, tiled=True)
+    with jax.named_scope("main"):
+        tapered = (raw_window * taper[None, :]).astype(jnp.bfloat16)
+        samples = lax.all_to_all(tapered.reshape(groups, channels, span), "gy", split_axis=0, concat_axis=0, tiled=True)
 
     twiddle = twiddle_table()
     upper, lower = inner_table()
-    table = inverse_table(core)
+    near0, away = whiten(core.reshape(1), first, twiddle, upper, lower)
+    near1 = shift(away, "core", 1)
+    ahead0, behind0 = shift(near0, "y", 1), shift(near0, "y", 3)
+    ahead1, behind1 = shift(near1, "y", 1), shift(near1, "y", 3)
+    far0, far1 = shift(ahead0, "y", 1), shift(behind1, "y", 3)
+
+    late, _ = lax.optimization_barrier((core, near0))
+    table = inverse_table(late)
 
     mine, other = whiten(core.reshape(1), samples, twiddle, upper, lower)
     sister = shift(other, "core", 1)
-    here = gx * groups + gy
-    local = source_ids - here * channels
-    own = jnp.take(mine, local, axis=0)
-    theirs = shift(jnp.take(other, local, axis=0), "core", 1)
-    block = jnp.stack([own, theirs], axis=0)
-    axes = ("x", "z", "y")
-    block = gather_ring(block, axes[0])
-    block = gather_ring(block, axes[1])
-    sources = gather_last(block, axes[2]).reshape(devices * 2, NSEG * HALF_ROWS, LANES)
-
-    device_no = source_no // 2
-    at = {"y": device_no // (2 * groups), "z": device_no % groups // SIDE, "x": device_no % SIDE}
-    core_at = device_no // groups % 2
-    source_at = 0
-    for axis in reversed(axes):
-        source_at = source_at * SIDE + (place[axis] - at[axis]) % SIDE
-    source_at = (source_at * 2 + (core_at ^ core)) * 2 + source_no % 2
-
-    partial = correlate(source_at, receiver_at, sources, mine, sister, table)
-    outgoing = jnp.transpose(partial.reshape(2, devices, 2, NLAG), (1, 0, 2, 3))
-    returned = lax.all_to_all(outgoing, ("gx", "gy"), split_axis=0, concat_axis=0, tiled=True)
+
+    dev = jnp.arange(devices, dtype=jnp.int32)
+    own = (
+        (((dev // 64) ^ core) + (place["y"] - dev // 16 % SIDE) % SIDE * 2) * groups
+        + (place["z"] - dev // SIDE % SIDE) % SIDE * SIDE
+        + (place["x"] - dev % SIDE) % SIDE
+    )
+    key = notes // (channels * 256)
+    low = notes % (channels * 256)
+    kinds = jnp.stack([here * 2, here * 2 + 1, (here ^ groups) * 2, (here ^ groups) * 2 + 1])
+    found = jnp.sum(jnp.where(key[None] == kinds[:, None, None], low[None] + 1, 0), axis=2)
+    asked = jnp.sum(jnp.where(own[None, None, :] == dev[None, :, None], found[:, None, :], 0), axis=2)
+    asked = jnp.transpose(asked.reshape(2, 2, devices), (2, 0, 1)).reshape(-1)
+    valid = asked > 0
+    asked = jnp.maximum(asked - 1, 0)
+    slots = asked.shape[0]
+    source_no = asked % 256
+    source_gx = source_no // (2 * groups)
+    rel_y = (place["y"] - source_gx // 2) % SIDE
+    source_at = (rel_y * 2 + (source_gx % 2 ^ core)) * (2 * groups) + source_no % (2 * groups)
+    slot_no = jnp.arange(slots, dtype=jnp.int32)
+    receiver_at = asked // 256 + slot_no // 2 % 2 * channels
+    spot = jnp.sum((valid[None, :] & (slot_no[None, :] < slot_no[:, None])).astype(jnp.int32), axis=1)
+    hit = valid[None, :] & (spot[None, :] == slot_no[:, None])
+    lists = jnp.sum(jnp.where(hit[None], jnp.stack([source_at, receiver_at, slot_no - slots])[:, None, :], 0), axis=2)
+    count = jnp.sum(valid.astype(jnp.int32)).reshape(1)
+
+    pieces = [near0, near1, ahead0, ahead1, far0, far1, behind0, behind1, mine, sister]
+    partial = correlate(count, lists[0], lists[1], lists[2] + slots, pieces, table)
+    with jax.named_scope("results"):
+        returned = lax.all_to_all(partial.reshape(devices, 4, NLAG), ("gx", "gy"), split_axis=0, concat_axis=0, tiled=True)
     returned = returned.reshape(devices * 4, NLAG)
-    holder_core = holder // groups % 2
     row = jnp.arange(4 * devices, dtype=jnp.int32)
     row_dev, row_rel, row_rank = row // 4, row // 2 % 2, row % 2
     row_holder = jnp.where(row_rel == 0, row_dev, row_dev ^ groups)

time: 180 us -> 173 us (0.961)
  other arithmetic: 30.5 us -> 16.2 us
  waiting for transfers between devices: 62.1 us -> 48.5 us
  starting transfers between devices: 50.8 us -> 62.7 us
  Pallas kernels: 20.5 us -> 25.8 us
  local copies, waits for them, and re-layouts: 11.9 us -> 14.9 us
    convert_element_type x1, other arithmetic: 17.2 us -> 0.08 us  [body(): (jnp.take(raw_window, wanted, axis=0) * taper[None, :]).astype(jnp.bfloat16)]
    all_to_all x1, waiting for transfers between devices: 27 us -> 11.8 us  [body(): lax.all_to_all(tapered.reshape(groups, channels, span), 'gy', split_axis=...]
    ppermute x4 -> x9, waiting for transfers between devices: 7.7 us -> 21.1 us  [shift(): lax.ppermute(value, 'gx', [(g, (g + 2 * step) % (2 * SIDE)) for g in rang...]
    ppermute x3 -> x6, waiting for transfers between devices: 11.6 us -> 2.7 us  [shift(): lax.ppermute(value, 'gy', [(g, (g + SIDE * step) % (SIDE * SIDE)) for g i...]
    ppermute x3 -> x6, starting transfers between devices: 3.02 us -> 11 us  [shift(): lax.ppermute(value, 'gy', [(g, (g + SIDE * step) % (SIDE * SIDE)) for g i...]
    all_to_all x2, starting transfers between devices: 24.1 us -> 16.3 us  [the longest x1 10.1 us: body(): lax.all_to_all(partial.reshape(devices, 4, NLAG), ('gx', 'gy'), split_axi...]
    ppermute x4 -> x9, starting transfers between devices: 6.03 us -> 12.4 us  [shift(): lax.ppermute(value, 'gx', [(g, (g + 2 * step) % (2 * SIDE)) for g in rang...]
    ppermute x3, starting transfers between devices: 3.92 us -> 9.6 us  [shift(): return lax.ppermute(value, 'gx', [(g, g ^ 1) for g in range(2 * SIDE)])]
  transfers between devices with their start and end apart: 16 -> 27, of which waited for: 10 -> 11; matrix products, arithmetic and copies ran while one was open for 15% -> 15% of each run, Pallas kernels for 0% -> 9%
where the time goes in v2:
time: 173 us; the launch traced here: 170 us
  starting transfers between devices  62.7 us (36%)
  waiting for transfers between devices  48.5 us (28%)
  Pallas kernels  25.8 us (15%)
  other arithmetic  16.2 us (9%)
  local copies, waits for them, and re-layouts  14.9 us (9%)
    ppermute x9, waiting for transfers between devices, shift(): lax.ppermute(value, 'gx', [(g, (g + 2 * step) % (2 * SIDE)) for g in rang...  21.1 us
    pallas_call x2, Pallas kernels, whiten(): pl.pallas_call(whiten_kernel, out_shape=(out, out), grid_spec=pltpu.Prefe...  15 us
    ppermute x9, starting transfers between devices, shift(): lax.ppermute(value, 'gx', [(g, (g + 2 * step) % (2 * SIDE)) for g in rang...  12.4 us
    all_to_all x1, waiting for transfers between devices, body(): lax.all_to_all(partial.reshape(devices, 4, NLAG), ('gx', 'gy'), split_axi...  12.1 us
    all_to_all x1, waiting for transfers between devices, body(): lax.all_to_all(tapered.reshape(groups, channels, span), 'gy', split_axis=...  11.8 us
    ppermute x6, starting transfers between devices, shift(): lax.ppermute(value, 'gy', [(g, (g + SIDE * step) % (SIDE * SIDE)) for g i...  11 us
    pallas_call x1, Pallas kernels, correlate(): pl.pallas_call(correlate_kernel, out_shape=jax.ShapeDtypeStruct((slots, N...  10.8 us
    all_to_all x1, starting transfers between devices, body(): lax.all_to_all(partial.reshape(devices, 4, NLAG), ('gx', 'gy'), split_axi...  10.1 us
  transfers between devices with their start and end apart: 27, of which 11 were waited for; matrix products, arithmetic and copies ran while one was open for 15% of the time, Pallas kernels for 9%

profile of v2, /device:TPU:5, one launch (start us, length us, event | category | flops | bytes accessed | tf_op | source)
XLA Modules:
  0.0 169.6 jit_solution(12340511040899139245)
XLA Ops:
  5.5 2.1 %collective-permute-start.1 = (s32[128]{0:T(128)S(1)}, s32[128]{0:T(128)S(1)}, u32[]{:S(2)}, u32[]{:S(2)}) collective-permute-start(s32[128]{0:T(128)S(1)} %multiply_add_fusion), channel_id=1, source_target_pairs={{0,2},{1,3},{2,0},{3,1},{4,6},{5,7},{6,4},{7,5},{8,10},{9,11},{10,... | collective-permute-start | bytes 1544 | tf_op jit(solution)/shard_map/requests/ppermute | solution.py:257
  9.7 4.1 %multiply_convert_fusion = bf16[1024,1024]{1,0:T(8,128)(2,1)} fusion(f32[1024,1024]{1,0:T(8,128)} %param.5, f32[1024]{0:T(1024)S(1)} %fusion.57), kind=kLoop, calls=%fused_computation.2 | loop fusion | flops 2097152 | bytes 6295552 | tf_op jit(solution)/shard_map/main/convert_element_type | solution.py:299
  13.9 1.8 %collective-permute-start.2 = (s32[128]{0:T(128)S(1)}, s32[128]{0:T(128)S(1)}, u32[]{:S(2)}, u32[]{:S(2)}) collective-permute-start(s32[128]{0:T(128)S(1)} %multiply_add_fusion), channel_id=1, source_target_pairs={{0,3},{1,0},{2,1},{3,2},{4,7},{5,4},{6,5},{7,6},{8,11},{9,8},{10,9... | collective-permute-start | bytes 1544 | tf_op jit(solution)/shard_map/requests/ppermute | solution.py:257
  15.7 1.7 %collective-permute-start.13 = (s32[4,2]{1,0:T(4,128)S(1)}, s32[4,2]{1,0:T(4,128)S(1)}, u32[]{:S(2)}, u32[]{:S(2)}) collective-permute-start(s32[4,2]{1,0:T(4,128)S(1)} %pad_add_fusion.6), channel_id=1, source_target_pairs={{0,4},{1,5},{2,6},{3,7},{4,8},{5,9},{6,10},{7,11},{8,12},{9,13},{1... | collective-permute-start | bytes 104 | tf_op jit(solution)/shard_map/ids/ppermute | solution.py:256
  17.4 3.3 %collective-permute-start.14 = (s32[4,2]{1,0:T(4,128)S(1)}, s32[4,2]{1,0:T(4,128)S(1)}, u32[]{:S(2)}, u32[]{:S(2)}) collective-permute-start(s32[4,2]{1,0:T(4,128)S(1)} %pad_add_fusion.6), channel_id=1, source_target_pairs={{0,8},{1,9},{2,10},{3,11},{4,12},{5,13},{6,14},{7,15},{8,0},{9,1},... | collective-permute-start | bytes 104 | tf_op jit(solution)/shard_map/ids/ppermute | solution.py:256
  20.8 1.2 collective-permute-start.15
  22.2 1.2 collective-permute-done.15
  24.3 2.9 %gather_fusion.1 = f32[32,1024]{1,0:T(8,128)S(1)} fusion(f32[1024,1024]{1,0:T(8,128)} %param.5, s32[1024]{0:T(1024)S(1)} %pad_clamp_fusion), kind=kCustom, calls=%fused_computation.1 | custom fusion | bytes 262272 | tf_op jit(solution)/shard_map/early/jit(_take)/gather | solution.py:295
  28.4 6.3 %all-to-all-start = ((bf16[16,32,1024]{2,1,0:T(8,128)(2,1)}), bf16[16,32,1024]{2,1,0:T(8,128)(2,1)S(1)}, u32[]{:S(2)}, u32[]{:S(2)}) async-start(bf16[16,32,1024]{2,1,0:T(8,128)(2,1)} %broadcast_in_dim.86), calls=%async_computation | async-start | bytes 2097152 | tf_op jit(solution)/shard_map/early/all_to_all | solution.py:297
  34.7 1.9 %fusion.16 = (f32[128,512]{1,0:T(8,128)S(1)}, f32[128,512]{1,0:T(8,128)}) fusion(s32[512]{0:T(512)S(1)} %add_select_fusion.8, s32[128]{0:T(128)S(1)} %broadcast_multiply_fusion.2), kind=kLoop, calls=%fused_computation.41 | loop fusion | flops 917504 | bytes 526848 | tf_op jit(solution)/shard_map/sin | solution.py:58
  36.7 1.3 collective-permute-start.3
  37.9 2.4 %collective-permute-start.4 = (s32[4,128]{1,0:T(4,128)S(1)}, s32[4,128]{1,0:T(4,128)S(1)}, u32[]{:S(2)}, u32[]{:S(2)}) collective-permute-start(s32[4,128]{1,0:T(4,128)S(1)} %get-tuple-element.47), channel_id=1, source_target_pairs={{0,8},{1,9},{2,10},{3,11},{4,12},{5,13},{6,14},{7,15},{8,0},{9,1},... | collective-permute-start | bytes 6152 | tf_op jit(solution)/shard_map/requests/ppermute | solution.py:256
  40.3 1.2 collective-permute-start.5
  43.1 1.3 collective-permute-start.6
  44.4 2.6 %collective-permute-start.7 = (s32[4,4,128]{2,1,0:T(4,128)S(1)}, s32[4,4,128]{2,1,0:T(4,128)S(1)}, u32[]{:S(2)}, u32[]{:S(2)}) collective-permute-start(s32[4,4,128]{2,1,0:T(4,128)S(1)} %get-tuple-element.35), channel_id=1, source_target_pairs={{0,64},{16,80},{32,96},{48,112},{64,0},{80,16},{96,32},{112,48},{1... | collective-permute-start | bytes 24584 | tf_op jit(solution)/shard_map/requests/ppermute | solution.py:254
  49.6 8.5 %collective-permute-start.9 = (s32[4,4,4,128]{3,2,1,0:T(4,128)S(1)}, s32[4,4,4,128]{3,2,1,0:T(4,128)S(1)}, u32[]{:S(2)}, u32[]{:S(2)}) collective-permute-start(s32[4,4,4,128]{3,2,1,0:T(4,128)S(1)} %get-tuple-element.30), channel_id=1, source_target_pairs={{0,16},{16,0},{32,48},{48,32},{64,80},{80,64},{96,112},{112,96},{1... | collective-permute-start | bytes 98312 | tf_op jit(solution)/shard_map/requests/ppermute | solution.py:252
  59.1 6.2 %all-to-all-start.1 = ((bf16[16,64,1024]{2,1,0:T(8,128)(2,1)}), bf16[16,64,1024]{2,1,0:T(8,128)(2,1)S(1)}, u32[]{:S(2)}, u32[]{:S(2)}) async-start(bf16[16,64,1024]{2,1,0:T(8,128)(2,1)} %bitcast.60), calls=%async_computation.1 | async-start | bytes 4194304 | tf_op jit(solution)/shard_map/main/all_to_all | solution.py:300
  71.2 1.2 copy-done.1
  72.4 5.6 %whiten.2 = (bf16[32,64,128]{2,1,0:T(8,128)(2,1)}, bf16[32,64,128]{2,1,0:T(8,128)(2,1)S(1)}) custom-call(s32[1]{0:T(128)} %bitcast.30.core_ref, bf16[16,32,1024]{2,1,0:T(8,128)(2,1)S(1)} %copy-done.1, f32[2,16,256]{2,1,0:T(8,128)S(1)} %pad_maximum_fusion.1.tw_ref, bf16[512,512]{1,0:T(8,128)(2,1)S(1)} %fusion.9.upper_ref, ...), custom_call_target="tpu_custom_call" | custom-call | tf_op jit(solution)/shard_map/whiten/pallas_call | solution.py:151
  80.3 2.3 %collective-permute-start.20 = (bf16[32,64,128]{2,1,0:T(8,128)(2,1)}, bf16[32,64,128]{2,1,0:T(8,128)(2,1)}, u32[]{:S(2)}, u32[]{:S(2)}) collective-permute-start(bf16[32,64,128]{2,1,0:T(8,128)(2,1)} %collective-permute-done.16.refs_1_), channel_id=1, source_target_pairs={{0,96},{16,112},{32,0},{48,16},{64,32},{80,48},{96,64},{112,80},{1... | collective-permute-start | bytes 1572872 | tf_op jit(solution)/shard_map/ppermute | solution.py:254
  82.6 11.8 %all-to-all-done.1.x_ref = bf16[16,64,1024]{2,1,0:T(8,128)(2,1)S(1)} async-done(((bf16[16,64,1024]{2,1,0:T(8,128)(2,1)}), bf16[16,64,1024]{2,1,0:T(8,128)(2,1)S(1)}, u32[]{:S(2)}, u32[]{:S(2)}) %all-to-all-start.1) | async-done | bytes 2097184 | tf_op jit(solution)/shard_map/main/all_to_all | solution.py:300
  94.4 9.4 %whiten.3 = (bf16[64,64,128]{2,1,0:T(8,128)(2,1)S(1)}, bf16[64,64,128]{2,1,0:T(8,128)(2,1)}) custom-call(s32[1]{0:T(128)} %bitcast.30.core_ref, bf16[16,64,1024]{2,1,0:T(8,128)(2,1)S(1)} %all-to-all-done.1.x_ref, f32[2,16,256]{2,1,0:T(8,128)S(1)} %pad_maximum_fusion.1.tw_ref, bf16[512,512]{1,0:T(8,128)(2,1)S(1)} %fusion.9.upper_ref, ...), custom_call_target="tpu_custom_call" | custom-call | tf_op jit(solution)/shard_map/whiten/pallas_call | solution.py:151
  105.3 2.3 %collective-permute-start.22 = (bf16[32,64,128]{2,1,0:T(8,128)(2,1)}, bf16[32,64,128]{2,1,0:T(8,128)(2,1)S(1)}, u32[]{:S(2)}, u32[]{:S(2)}) collective-permute-start(bf16[32,64,128]{2,1,0:T(8,128)(2,1)} %get-tuple-element.14.refs_0_), channel_id=1, source_target_pairs={{0,96},{16,112},{32,0},{48,16},{64,32},{80,48},{96,64},{112,80},{1... | collective-permute-start | bytes 1572872 | tf_op jit(solution)/shard_map/ppermute | solution.py:254
  107.9 2.7 %collective-permute-start.21 = (bf16[32,64,128]{2,1,0:T(8,128)(2,1)}, bf16[32,64,128]{2,1,0:T(8,128)(2,1)S(1)}, u32[]{:S(2)}, u32[]{:S(2)}) collective-permute-start(bf16[32,64,128]{2,1,0:T(8,128)(2,1)} %collective-permute-done.20.refs_7_), channel_id=1, source_target_pairs={{0,96},{16,112},{32,0},{48,16},{64,32},{80,48},{96,64},{112,80},{1... | collective-permute-start | bytes 1572872 | tf_op jit(solution)/shard_map/ppermute | solution.py:254
  110.6 1.7 %multiply_convert_fusion.2 = (bf16[1,8,128,512]{3,2,1,0:T(8,128)(2,1)S(1)}, bf16[1,8,128,512]{3,2,1,0:T(8,128)(2,1)S(1)}) fusion(f32[128,512]{1,0:T(8,128)S(1)} %get-tuple-element.22, f32[8,512]{1,0:T(8,128)S(1)} %get-tuple-element.21, f32[128,512]{1,0:T(8,128)} %get-tuple-element.20, f32[8,512]{1,0:T(8,128)S(1)} %get-tuple-element.19, ...), kind=kLoop, calls=%fused_computation.6 | loop fusion | flops 5242880 | bytes 2662400 | tf_op jit(solution)/shard_map/convert
  112.3 1.5 pad_maximum_fusion
  113.9 5.2 %collective-permute-done.22.refs_6_ = bf16[32,64,128]{2,1,0:T(8,128)(2,1)S(1)} collective-permute-done((bf16[32,64,128]{2,1,0:T(8,128)(2,1)}, bf16[32,64,128]{2,1,0:T(8,128)(2,1)S(1)}, u32[]{:S(2)}, u32[]{:S(2)}) %collective-permute-start.22) | collective-permute-done | bytes 524320 | tf_op jit(solution)/shard_map/ppermute | solution.py:254
  119.1 3.3 %collective-permute-done.18.refs_3_ = bf16[32,64,128]{2,1,0:T(8,128)(2,1)S(1)} collective-permute-done((bf16[32,64,128]{2,1,0:T(8,128)(2,1)}, bf16[32,64,128]{2,1,0:T(8,128)(2,1)S(1)}, u32[]{:S(2)}, u32[]{:S(2)}) %collective-permute-start.18) | collective-permute-done | bytes 524320 | tf_op jit(solution)/shard_map/ppermute | solution.py:254
  122.3 11.2 %collective-permute-done.19.refs_4_ = bf16[32,64,128]{2,1,0:T(8,128)(2,1)S(1)} collective-permute-done((bf16[32,64,128]{2,1,0:T(8,128)(2,1)}, bf16[32,64,128]{2,1,0:T(8,128)(2,1)S(1)}, u32[]{:S(2)}, u32[]{:S(2)}) %collective-permute-start.19) | collective-permute-done | bytes 524320 | tf_op jit(solution)/shard_map/ppermute | solution.py:254
  134.6 10.8 %correlate.1 = bf16[512,512]{1,0:T(8,128)(2,1)S(1)} custom-call(s32[1]{0:T(128)} %bitcast.20.count_ref, s32[512]{0:T(512)S(1)} %bitcast.58, s32[512]{0:T(512)S(1)} %bitcast.57, s32[512]{0:T(512)S(1)} %bitcast.56, bf16[32,64,128]{2,1,0:T(8,128)(2,1)} %get-tuple-element.14.refs_0_, bf16[32,64,128]{2,1,0:T(8,128)(2,1)} %collective-permute-done.16.refs_1_, ...), custom_call_target="tpu_custom_call" | custom-call | tf_op jit(solution)/shard_map/correlate/pallas_call | solution.py:230
  146.3 10.1 %all-to-all-start.2 = ((bf16[128,4,512]{2,1,0:T(4,128)(2,1)}), bf16[128,4,512]{2,1,0:T(4,128)(2,1)S(1)}, u32[]{:S(2)}, u32[]{:S(2)}) async-start(bf16[128,4,512]{2,1,0:T(4,128)(2,1)} %reshape.1029), calls=%async_computation.2 | async-start | bytes 1048576 | tf_op jit(solution)/shard_map/results/all_to_all | solution.py:345
  156.4 12.1 %all-to-all-done.2 = bf16[128,4,512]{2,1,0:T(4,128)(2,1)S(1)} async-done(((bf16[128,4,512]{2,1,0:T(4,128)(2,1)}), bf16[128,4,512]{2,1,0:T(4,128)(2,1)S(1)}, u32[]{:S(2)}, u32[]{:S(2)}) %all-to-all-start.2) | async-done | bytes 524320 | tf_op jit(solution)/shard_map/results/all_to_all | solution.py:345
  (122 shorter events, 28.2 us)
Async XLA Ops:
  0.7 13.2 %collective-permute-start.10 = (s32[2]{0:T(128)S(1)}, s32[2]{0:T(128)S(1)}, u32[]{:S(2)}, u32[]{:S(2)}) collective-permute-start(s32[2]{0:T(128)S(1)} %broadcast_subtract_fusion.1), channel_id=1, source_target_pairs={{0,1},{1,2},{2,3},{3,0},{4,5},{5,6},{6,7},{7,4},{8,9},{9,10},{10,1... | collective-permute-start | bytes 32 | tf_op jit(solution)/shard_map/ids/ppermute | solution.py:257
  1.6 14.1 %collective-permute-start.11 = (s32[2]{0:T(128)S(1)}, s32[2]{0:T(128)S(1)}, u32[]{:S(2)}, u32[]{:S(2)}) collective-permute-start(s32[2]{0:T(128)S(1)} %broadcast_subtract_fusion.1), channel_id=1, source_target_pairs={{0,2},{1,3},{2,0},{3,1},{4,6},{5,7},{6,4},{7,5},{8,10},{9,11},{10,... | collective-permute-start | bytes 32 | tf_op jit(solution)/shard_map/ids/ppermute | solution.py:257
  2.1 13.6 %collective-permute-start.12 = (s32[2]{0:T(128)S(1)}, s32[2]{0:T(128)S(1)}, u32[]{:S(2)}, u32[]{:S(2)}) collective-permute-start(s32[2]{0:T(128)S(1)} %broadcast_subtract_fusion.1), channel_id=1, source_target_pairs={{0,3},{1,0},{2,1},{3,2},{4,7},{5,4},{6,5},{7,6},{8,11},{9,8},{10,9... | collective-permute-start | bytes 32 | tf_op jit(solution)/shard_map/ids/ppermute | solution.py:257
  4.4 32.3 %collective-permute-start = (s32[128]{0:T(128)S(1)}, s32[128]{0:T(128)S(1)}, u32[]{:S(2)}, u32[]{:S(2)}) collective-permute-start(s32[128]{0:T(128)S(1)} %multiply_add_fusion), channel_id=1, source_target_pairs={{0,1},{1,2},{2,3},{3,0},{4,5},{5,6},{6,7},{7,4},{8,9},{9,10},{10,1... | collective-permute-start | bytes 1544 | tf_op jit(solution)/shard_map/requests/ppermute | solution.py:257
  5.5 31.1 %collective-permute-start.1 = (s32[128]{0:T(128)S(1)}, s32[128]{0:T(128)S(1)}, u32[]{:S(2)}, u32[]{:S(2)}) collective-permute-start(s32[128]{0:T(128)S(1)} %multiply_add_fusion), channel_id=1, source_target_pairs={{0,2},{1,3},{2,0},{3,1},{4,6},{5,7},{6,4},{7,5},{8,10},{9,11},{10,... | collective-permute-start | bytes 1544 | tf_op jit(solution)/shard_map/requests/ppermute | solution.py:257
  8.3 26.4 %copy-start.5 = (s32[512]{0:T(512)}, s32[512]{0:T(512)S(1)}, u32[]{:S(2)}) copy-start(s32[512]{0:T(512)S(1)} %add_select_fusion.8) | copy-start | bytes 6148
  13.9 22.8 %collective-permute-start.2 = (s32[128]{0:T(128)S(1)}, s32[128]{0:T(128)S(1)}, u32[]{:S(2)}, u32[]{:S(2)}) collective-permute-start(s32[128]{0:T(128)S(1)} %multiply_add_fusion), channel_id=1, source_target_pairs={{0,3},{1,0},{2,1},{3,2},{4,7},{5,4},{6,5},{7,6},{8,11},{9,8},{10,9... | collective-permute-start | bytes 1544 | tf_op jit(solution)/shard_map/requests/ppermute | solution.py:257
  15.7 5.1 %collective-permute-start.13 = (s32[4,2]{1,0:T(4,128)S(1)}, s32[4,2]{1,0:T(4,128)S(1)}, u32[]{:S(2)}, u32[]{:S(2)}) collective-permute-start(s32[4,2]{1,0:T(4,128)S(1)} %pad_add_fusion.6), channel_id=1, source_target_pairs={{0,4},{1,5},{2,6},{3,7},{4,8},{5,9},{6,10},{7,11},{8,12},{9,13},{1... | collective-permute-start | bytes 104 | tf_op jit(solution)/shard_map/ids/ppermute | solution.py:256
  17.4 4.7 %collective-permute-start.14 = (s32[4,2]{1,0:T(4,128)S(1)}, s32[4,2]{1,0:T(4,128)S(1)}, u32[]{:S(2)}, u32[]{:S(2)}) collective-permute-start(s32[4,2]{1,0:T(4,128)S(1)} %pad_add_fusion.6), channel_id=1, source_target_pairs={{0,8},{1,9},{2,10},{3,11},{4,12},{5,13},{6,14},{7,15},{8,0},{9,1},... | collective-permute-start | bytes 104 | tf_op jit(solution)/shard_map/ids/ppermute | solution.py:256
  20.8 2.5 %collective-permute-start.15 = (s32[4,2]{1,0:T(4,128)S(1)}, s32[4,2]{1,0:T(4,128)S(1)}, u32[]{:S(2)}, u32[]{:S(2)}) collective-permute-start(s32[4,2]{1,0:T(4,128)S(1)} %pad_add_fusion.6), channel_id=1, source_target_pairs={{0,12},{1,13},{2,14},{3,15},{4,0},{5,1},{6,2},{7,3},{8,4},{9,5},{1... | collective-permute-start | bytes 104 | tf_op jit(solution)/shard_map/ids/ppermute | solution.py:256
  28.4 29.6 %all-to-all-start = ((bf16[16,32,1024]{2,1,0:T(8,128)(2,1)}), bf16[16,32,1024]{2,1,0:T(8,128)(2,1)S(1)}, u32[]{:S(2)}, u32[]{:S(2)}) async-start(bf16[16,32,1024]{2,1,0:T(8,128)(2,1)} %broadcast_in_dim.86), calls=%async_computation | async-start | bytes 2097152 | tf_op jit(solution)/shard_map/early/all_to_all | solution.py:297
  34.7 24.4 %copy-start.10 = (s32[128]{0:T(128)}, s32[128]{0:T(128)S(1)}, u32[]{:S(2)}) copy-start(s32[128]{0:T(128)S(1)} %broadcast_multiply_fusion.2) | copy-start | bytes 1540
  36.7 4.9 %collective-permute-start.3 = (s32[4,128]{1,0:T(4,128)S(1)}, s32[4,128]{1,0:T(4,128)S(1)}, u32[]{:S(2)}, u32[]{:S(2)}) collective-permute-start(s32[4,128]{1,0:T(4,128)S(1)} %get-tuple-element.47), channel_id=1, source_target_pairs={{0,4},{1,5},{2,6},{3,7},{4,8},{5,9},{6,10},{7,11},{8,12},{9,13},{1... | collective-permute-start | bytes 6152 | tf_op jit(solution)/shard_map/requests/ppermute | solution.py:256
  37.9 4.8 %collective-permute-start.4 = (s32[4,128]{1,0:T(4,128)S(1)}, s32[4,128]{1,0:T(4,128)S(1)}, u32[]{:S(2)}, u32[]{:S(2)}) collective-permute-start(s32[4,128]{1,0:T(4,128)S(1)} %get-tuple-element.47), channel_id=1, source_target_pairs={{0,8},{1,9},{2,10},{3,11},{4,12},{5,13},{6,14},{7,15},{8,0},{9,1},... | collective-permute-start | bytes 6152 | tf_op jit(solution)/shard_map/requests/ppermute | solution.py:256
  40.3 2.8 %collective-permute-start.5 = (s32[4,128]{1,0:T(4,128)S(1)}, s32[4,128]{1,0:T(4,128)S(1)}, u32[]{:S(2)}, u32[]{:S(2)}) collective-permute-start(s32[4,128]{1,0:T(4,128)S(1)} %get-tuple-element.47), channel_id=1, source_target_pairs={{0,12},{1,13},{2,14},{3,15},{4,0},{5,1},{6,2},{7,3},{8,4},{9,5},{1... | collective-permute-start | bytes 6152 | tf_op jit(solution)/shard_map/requests/ppermute | solution.py:256
  43.1 5.0 %collective-permute-start.6 = (s32[4,4,128]{2,1,0:T(4,128)S(1)}, s32[4,4,128]{2,1,0:T(4,128)S(1)}, u32[]{:S(2)}, u32[]{:S(2)}) collective-permute-start(s32[4,4,128]{2,1,0:T(4,128)S(1)} %get-tuple-element.35), channel_id=1, source_target_pairs={{0,32},{16,48},{32,64},{48,80},{64,96},{80,112},{96,0},{112,16},{1... | collective-permute-start | bytes 24584 | tf_op jit(solution)/shard_map/requests/ppermute | solution.py:254
  44.4 4.3 %collective-permute-start.7 = (s32[4,4,128]{2,1,0:T(4,128)S(1)}, s32[4,4,128]{2,1,0:T(4,128)S(1)}, u32[]{:S(2)}, u32[]{:S(2)}) collective-permute-start(s32[4,4,128]{2,1,0:T(4,128)S(1)} %get-tuple-element.35), channel_id=1, source_target_pairs={{0,64},{16,80},{32,96},{48,112},{64,0},{80,16},{96,32},{112,48},{1... | collective-permute-start | bytes 24584 | tf_op jit(solution)/shard_map/requests/ppermute | solution.py:254
  47.1 2.5 %collective-permute-start.8 = (s32[4,4,128]{2,1,0:T(4,128)S(1)}, s32[4,4,128]{2,1,0:T(4,128)S(1)}, u32[]{:S(2)}, u32[]{:S(2)}) collective-permute-start(s32[4,4,128]{2,1,0:T(4,128)S(1)} %get-tuple-element.35), channel_id=1, source_target_pairs={{0,96},{16,112},{32,0},{48,16},{64,32},{80,48},{96,64},{112,80},{1... | collective-permute-start | bytes 24584 | tf_op jit(solution)/shard_map/requests/ppermute | solution.py:254
  49.6 15.8 %collective-permute-start.9 = (s32[4,4,4,128]{3,2,1,0:T(4,128)S(1)}, s32[4,4,4,128]{3,2,1,0:T(4,128)S(1)}, u32[]{:S(2)}, u32[]{:S(2)}) collective-permute-start(s32[4,4,4,128]{3,2,1,0:T(4,128)S(1)} %get-tuple-element.30), channel_id=1, source_target_pairs={{0,16},{16,0},{32,48},{48,32},{64,80},{80,64},{96,112},{112,96},{1... | collective-permute-start | bytes 98312 | tf_op jit(solution)/shard_map/requests/ppermute | solution.py:252
  59.1 35.3 %all-to-all-start.1 = ((bf16[16,64,1024]{2,1,0:T(8,128)(2,1)}), bf16[16,64,1024]{2,1,0:T(8,128)(2,1)S(1)}, u32[]{:S(2)}, u32[]{:S(2)}) async-start(bf16[16,64,1024]{2,1,0:T(8,128)(2,1)} %bitcast.60), calls=%async_computation.1 | async-start | bytes 4194304 | tf_op jit(solution)/shard_map/main/all_to_all | solution.py:300
  78.1 29.5 %copy-start.6 = (s32[512]{0:T(512)S(1)}, s32[512]{0:T(512)}, u32[]{:S(2)}) copy-start(s32[512]{0:T(512)} %copy-done.5) | copy-start | bytes 6148
  78.1 32.5 %copy-start.11 = (s32[128]{0:T(128)S(1)}, s32[128]{0:T(128)}, u32[]{:S(2)}) copy-start(s32[128]{0:T(128)} %copy-done.10) | copy-start | bytes 1540
  78.1 2.2 %collective-permute-start.16 = (bf16[32,64,128]{2,1,0:T(8,128)(2,1)S(1)}, bf16[32,64,128]{2,1,0:T(8,128)(2,1)}, u32[]{:S(2)}, u32[]{:S(2)}) collective-permute-start(bf16[32,64,128]{2,1,0:T(8,128)(2,1)S(1)} %get-tuple-element.15), channel_id=1, source_target_pairs={{0,16},{16,0},{32,48},{48,32},{64,80},{80,64},{96,112},{112,96},{1... | collective-permute-start | bytes 1572872 | tf_op jit(solution)/shard_map/ppermute | solution.py:252
  79.4 28.4 %collective-permute-start.17 = (bf16[32,64,128]{2,1,0:T(8,128)(2,1)}, bf16[32,64,128]{2,1,0:T(8,128)(2,1)}, u32[]{:S(2)}, u32[]{:S(2)}) collective-permute-start(bf16[32,64,128]{2,1,0:T(8,128)(2,1)} %get-tuple-element.14.refs_0_), channel_id=1, source_target_pairs={{0,32},{16,48},{32,64},{48,80},{64,96},{80,112},{96,0},{112,16},{1... | collective-permute-start | bytes 1572872 | tf_op jit(solution)/shard_map/ppermute | solution.py:254
  80.3 27.5 %collective-permute-start.20 = (bf16[32,64,128]{2,1,0:T(8,128)(2,1)}, bf16[32,64,128]{2,1,0:T(8,128)(2,1)}, u32[]{:S(2)}, u32[]{:S(2)}) collective-permute-start(bf16[32,64,128]{2,1,0:T(8,128)(2,1)} %collective-permute-done.16.refs_1_), channel_id=1, source_target_pairs={{0,96},{16,112},{32,0},{48,16},{64,32},{80,48},{96,64},{112,80},{1... | collective-permute-start | bytes 1572872 | tf_op jit(solution)/shard_map/ppermute | solution.py:254
  104.7 28.8 %collective-permute-start.23 = (bf16[64,64,128]{2,1,0:T(8,128)(2,1)}, bf16[64,64,128]{2,1,0:T(8,128)(2,1)S(1)}, u32[]{:S(2)}, u32[]{:S(2)}) collective-permute-start(bf16[64,64,128]{2,1,0:T(8,128)(2,1)} %get-tuple-element.17), channel_id=1, source_target_pairs={{0,16},{16,0},{32,48},{48,32},{64,80},{80,64},{96,112},{112,96},{1... | collective-permute-start | bytes 3145736 | tf_op jit(solution)/shard_map/ppermute | solution.py:252
  105.3 13.8 %collective-permute-start.22 = (bf16[32,64,128]{2,1,0:T(8,128)(2,1)}, bf16[32,64,128]{2,1,0:T(8,128)(2,1)S(1)}, u32[]{:S(2)}, u32[]{:S(2)}) collective-permute-start(bf16[32,64,128]{2,1,0:T(8,128)(2,1)} %get-tuple-element.14.refs_0_), channel_id=1, source_target_pairs={{0,96},{16,112},{32,0},{48,16},{64,32},{80,48},{96,64},{112,80},{1... | collective-permute-start | bytes 1572872 | tf_op jit(solution)/shard_map/ppermute | solution.py:254
  107.7 14.6 %collective-permute-start.18 = (bf16[32,64,128]{2,1,0:T(8,128)(2,1)}, bf16[32,64,128]{2,1,0:T(8,128)(2,1)S(1)}, u32[]{:S(2)}, u32[]{:S(2)}) collective-permute-start(bf16[32,64,128]{2,1,0:T(8,128)(2,1)} %collective-permute-done.16.refs_1_), channel_id=1, source_target_pairs={{0,32},{16,48},{32,64},{48,80},{64,96},{80,112},{96,0},{112,16},{1... | collective-permute-start | bytes 1572872 | tf_op jit(solution)/shard_map/ppermute | solution.py:254
  107.8 25.8 %collective-permute-start.19 = (bf16[32,64,128]{2,1,0:T(8,128)(2,1)}, bf16[32,64,128]{2,1,0:T(8,128)(2,1)S(1)}, u32[]{:S(2)}, u32[]{:S(2)}) collective-permute-start(bf16[32,64,128]{2,1,0:T(8,128)(2,1)} %collective-permute-done.17.refs_2_), channel_id=1, source_target_pairs={{0,32},{16,48},{32,64},{48,80},{64,96},{80,112},{96,0},{112,16},{1... | collective-permute-start | bytes 1572872 | tf_op jit(solution)/shard_map/ppermute | solution.py:254
  107.9 25.7 %collective-permute-start.21 = (bf16[32,64,128]{2,1,0:T(8,128)(2,1)}, bf16[32,64,128]{2,1,0:T(8,128)(2,1)S(1)}, u32[]{:S(2)}, u32[]{:S(2)}) collective-permute-start(bf16[32,64,128]{2,1,0:T(8,128)(2,1)} %collective-permute-done.20.refs_7_), channel_id=1, source_target_pairs={{0,96},{16,112},{32,0},{48,16},{64,32},{80,48},{96,64},{112,80},{1... | collective-permute-start | bytes 1572872 | tf_op jit(solution)/shard_map/ppermute | solution.py:254
  145.4 23.2 %copy-start.7 = (s32[128,1]{0,1:T(1,128)S(1)}, s32[128,1]{0,1:T(1,128)}, u32[]{:S(2)}) copy-start(s32[128,1]{0,1:T(1,128)} %param.8) | copy-start | bytes 1540
  146.3 22.2 %all-to-all-start.2 = ((bf16[128,4,512]{2,1,0:T(4,128)(2,1)}), bf16[128,4,512]{2,1,0:T(4,128)(2,1)S(1)}, u32[]{:S(2)}, u32[]{:S(2)}) async-start(bf16[128,4,512]{2,1,0:T(4,128)(2,1)} %reshape.1029), calls=%async_computation.2 | async-start | bytes 1048576 | tf_op jit(solution)/shard_map/results/all_to_all | solution.py:345
  (7 other events, 59.8 us)
